TPU v7x, 512 devices: a whole 4x4x16 slice. The times are simulated.
512 devices in a mesh: occ: 16 (over x, y_hi, core), virt: 32 (over y_lo, z).
Axes of the slice: x: 4, y: 4 (y_hi: 2, y_lo: 2; y = y_hi * 2 + y_lo), z: 16, core: 2. Of those that a mesh axis runs over, the one named last changes fastest.
Arguments:
- integrals: bfloat16 [192, 1024, 2048], P('occ', 'virt'), may hold values from -1 to 1
- occ_energy: float32 [192], replicated, may hold values from -2 to -0.5
- virt_energy: float32 [1024], replicated, may hold values from 0.2 to 3
- partners: int32 [2], replicated, may hold values from 0 to 191
Outputs:
- gamma: bfloat16 [192, 1024, 2048], P('occ', 'virt')
All inputs are finite; a program needn't handle non-finite values.
Results may differ from a plain program's by a relative error of at most 0.0043.
Values may be sent and summed in bfloat16 or wider, within the bound.
A program may use at most 64 MiB of HBM per device.

v0:
```python
import jax
import jax.numpy as jnp
from jax import lax
from jax.sharding import PartitionSpec as P


def broadcast(value, axis, source):
    kept = jnp.where(lax.axis_index(axis) == source, value, 0).astype(value.dtype)
    return lax.psum(kept, axis)


def passed_along(shard, axis, by):
    count = lax.axis_size(axis)
    return lax.ppermute(shard, axis, [(i, (i + by) % count) for i in range(count)])


def per_device(integrals, occ_energy, virt_energy, partners):
    occ_dev, local_virt, aux_width = integrals.shape
    n_virt = lax.axis_size("virt")
    whole_virt = local_virt * n_virt
    group_index = lax.axis_index("occ")
    my_index = lax.axis_index("virt")
    own_energy = lax.dynamic_slice_in_dim(occ_energy, group_index * occ_dev, occ_dev)
    local_energy = lax.dynamic_slice_in_dim(virt_energy, my_index * local_virt, local_virt)
    orbital_ids = jnp.arange(occ_energy.shape[0], dtype=jnp.int32)
    step_count = partners.shape[0]

    def fetch_partner(step_index):
        partner = partners[step_index]
        partner_local = lax.dynamic_index_in_dim(integrals, partner % occ_dev, 0, keepdims=False)
        partner_block = broadcast(partner_local, "occ", partner // occ_dev)
        pair_energy = jnp.sum(jnp.where(orbital_ids == partner, occ_energy, 0.0))
        return (partner_block, pair_energy)

    def place(state_now, piece_rows, offset):
        scores, whole_block = state_now
        columns = jnp.einsum(
            "iap,srp->siar", integrals, piece_rows, preferred_element_type=jnp.float32
        )
        scores = lax.dynamic_update_slice_in_dim(scores, columns, offset, 3)
        whole_block = lax.dynamic_update_slice_in_dim(whole_block, piece_rows, offset, 1)
        return (scores, whole_block)

    def collect(stacked):
        count = stacked.shape[0]
        initial = (
            jnp.zeros((count, occ_dev, local_virt, whole_virt), jnp.float32),
            jnp.zeros((count, whole_virt, aux_width), jnp.bfloat16),
        )

        def visit(turn_index, loop_state):
            state_now, pieces = loop_state
            source = (my_index - turn_index) % n_virt
            state_now = place(state_now, pieces, source * local_virt)
            pieces = passed_along(pieces, "virt", 1)
            return (state_now, pieces)

        state_now, pieces = lax.fori_loop(0, n_virt - 1, visit, (initial, stacked))
        source = (my_index - (n_virt - 1)) % n_virt
        return place(state_now, pieces, source * local_virt)

    fetched = [fetch_partner(step_index) for step_index in range(step_count)]
    gamma_sum = jnp.zeros(integrals.shape, jnp.float32)
    for item in fetched:
        scores, whole_block = collect(item[0][None])
        denominator = (
            local_energy[None, None, :, None]
            + virt_energy[None, None, None, :]
            - own_energy[None, :, None, None]
            - item[1][None][:, None, None, None]
        )
        amplitudes = (scores / denominator).astype(jnp.bfloat16)
        gamma_sum = gamma_sum + jnp.einsum(
            "siab,sbp->iap", amplitudes, whole_block, preferred_element_type=jnp.float32
        )
    return gamma_sum.astype(jnp.bfloat16)


def solution(mesh):
    in_specs = (P("occ", "virt", None), P(), P(), P())
    out_specs = P("occ", "virt", None)
    return jax.shard_map(
        per_device, mesh=mesh, in_specs=in_specs, out_specs=out_specs, check_vma=False
    )
```

profile of v0, /device:TPU:8, one launch (start us, length us, event | category | flops | bytes accessed | tf_op | source)
XLA Modules:
  0.0 775.1 jit_solution(10083200019153686629)
XLA Ops:
  18.5 153.7 %all-reduce.3.cloned.1.call-done = (bf16[1,32,2048]{2,1,0:T(8,128)(2,1)}, bf16[1,32,2048]{2,1,0:T(8,128)(2,1)}) async-done(((bf16[1,32,2048]{2,1,0:T(8,128)(2,1)}, bf16[1,32,2048]{2,1,0:T(8,128)(2,1)}), (bf16[1,32,2048]{2,1,0:T(8,128)(2,1)}, bf16[1,32,2048]{2,1,0:T(8,128)(2,1)})) %all-reduce.3.cloned.1.call-update) | async-done | bytes 262160 | tf_op jit(solution)/shard_map/psum | solution.py:9
  176.7 285.3 %while.39 = (s32[]{:T(128)}, f32[1,12,32,1024]{3,2,1,0:T(8,128)}, bf16[1,1024,2048]{2,1,0:T(8,128)(2,1)}, bf16[1,32,2048]{2,1,0:T(8,128)(2,1)S(1)}, bf16[12,32,2...) while((s32[]{:T(128)}, f32[1,12,32,1024]{3,2,1,0:T(8,128)}, ...), condition=%wide.region_6.7_spmd, body=%wide.region_5.6_spmd.sunk | while | flops 50331648 | bytes 2900292 | solution.py:58
  189.0 3.5 dynamic_update_slice.69
  197.9 3.5 dynamic_update_slice.69
  206.9 3.5 dynamic_update_slice.69
  218.3 4.0 collective-permute-done.1
  224.9 3.5 dynamic_update_slice.69
  233.9 3.5 dynamic_update_slice.69
  243.8 3.5 dynamic_update_slice.69
  256.4 4.3 collective-permute-done.1
  263.2 3.5 dynamic_update_slice.69
  272.2 3.5 dynamic_update_slice.69
  281.2 3.5 dynamic_update_slice.69
  292.6 4.0 collective-permute-done.1
  299.2 3.5 dynamic_update_slice.69
  308.3 3.5 dynamic_update_slice.69
  312.5 3.6 collective-permute-done.1
  318.6 3.5 dynamic_update_slice.69
  330.5 4.0 collective-permute-done.1
  366.4 4.1 collective-permute-done.1
  373.0 3.5 dynamic_update_slice.69
  383.0 3.5 dynamic_update_slice.69
  392.7 3.5 dynamic_update_slice.69
  404.1 4.0 collective-permute-done.1
  410.6 3.5 dynamic_update_slice.69
  419.6 3.5 dynamic_update_slice.69
  428.6 3.5 dynamic_update_slice.69
  440.0 4.0 collective-permute-done.1
  446.6 3.5 dynamic_update_slice.69
  455.5 3.5 dynamic_update_slice.69
  467.1 283.6 %while.38 = (s32[]{:T(128)}, f32[1,12,32,1024]{3,2,1,0:T(8,128)}, bf16[1,1024,2048]{2,1,0:T(8,128)(2,1)}, bf16[1,32,2048]{2,1,0:T(8,128)(2,1)S(1)}, bf16[12,32,2...) while((s32[]{:T(128)}, f32[1,12,32,1024]{3,2,1,0:T(8,128)}, ...), condition=%wide.region_2.3_spmd, body=%wide.region_1.2_spmd.sunk | while | flops 50331648 | bytes 2900292 | solution.py:58
  472.1 4.0 collective-permute-done
  478.6 3.5 dynamic_update_slice.67
  487.6 3.5 dynamic_update_slice.67
  496.6 3.5 dynamic_update_slice.67
  508.0 5.1 collective-permute-done
  515.7 3.5 dynamic_update_slice.67
  525.2 3.5 dynamic_update_slice.67
  534.2 3.5 dynamic_update_slice.67
  545.7 4.0 collective-permute-done
  552.2 3.5 dynamic_update_slice.67
  561.2 3.5 dynamic_update_slice.67
  570.2 3.5 dynamic_update_slice.67
  582.6 4.6 collective-permute-done
  589.8 3.5 dynamic_update_slice.67
  598.8 3.5 dynamic_update_slice.67
  607.8 3.5 dynamic_update_slice.67
  619.2 4.0 collective-permute-done
  638.2 3.9 collective-permute-done
  648.2 3.6 collective-permute-done
  656.7 4.1 collective-permute-done
  663.3 3.5 dynamic_update_slice.67
  672.3 3.5 dynamic_update_slice.67
  681.3 3.5 dynamic_update_slice.67
  692.7 4.0 collective-permute-done
  699.3 3.5 dynamic_update_slice.67
  708.2 3.5 dynamic_update_slice.67
  717.2 3.5 dynamic_update_slice.67
  728.7 4.0 collective-permute-done
  735.2 3.5 dynamic_update_slice.67
  744.2 3.5 dynamic_update_slice.67
  752.6 3.6 dynamic_update_slice.56
  759.1 5.4 fusion.2
  764.5 3.7 add_convert_fusion
  (340 shorter events, 374.0 us)
Async XLA Ops:
  6.5 165.7 %all-reduce.3.cloned.1.call-start = ((), (), s32[]{:S(2)}) async-start(), calls=%async_computation | async-start | bytes 524288 | tf_op jit(solution)/shard_map/psum | solution.py:9
  176.7 9.7 %collective-permute-start.1 = (bf16[1,32,2048]{2,1,0:T(8,128)(2,1)S(1)}, bf16[1,32,2048]{2,1,0:T(8,128)(2,1)S(1)}, u32[]{:S(2)}, u32[]{:S(2)}) collective-permute-start(bf16[1,32,2048]{2,1,0:T(8,128)(2,1)S(1)} %copy.18), channel_id=1, source_target_pairs={{0,1},{1,2},{2,3},{3,4},{4,5},{5,6},{6,7},{7,8},{8,9},{9,10},{10,1... | collective-permute-start | bytes 393224 | tf_op jit(solution)/shard_map/while/body/eval_jaxpr/ppermute | solution.py:14
  186.4 9.0 %collective-permute-start.1 = (bf16[1,32,2048]{2,1,0:T(8,128)(2,1)S(1)}, bf16[1,32,2048]{2,1,0:T(8,128)(2,1)S(1)}, u32[]{:S(2)}, u32[]{:S(2)}) collective-permute-start(bf16[1,32,2048]{2,1,0:T(8,128)(2,1)S(1)} %copy.18), channel_id=1, source_target_pairs={{0,1},{1,2},{2,3},{3,4},{4,5},{5,6},{6,7},{7,8},{8,9},{9,10},{10,1... | collective-permute-start | bytes 393224 | tf_op jit(solution)/shard_map/while/body/eval_jaxpr/ppermute | solution.py:14
  195.4 9.0 %collective-permute-start.1 = (bf16[1,32,2048]{2,1,0:T(8,128)(2,1)S(1)}, bf16[1,32,2048]{2,1,0:T(8,128)(2,1)S(1)}, u32[]{:S(2)}, u32[]{:S(2)}) collective-permute-start(bf16[1,32,2048]{2,1,0:T(8,128)(2,1)S(1)} %copy.18), channel_id=1, source_target_pairs={{0,1},{1,2},{2,3},{3,4},{4,5},{5,6},{6,7},{7,8},{8,9},{9,10},{10,1... | collective-permute-start | bytes 393224 | tf_op jit(solution)/shard_map/while/body/eval_jaxpr/ppermute | solution.py:14
  204.4 9.0 %collective-permute-start.1 = (bf16[1,32,2048]{2,1,0:T(8,128)(2,1)S(1)}, bf16[1,32,2048]{2,1,0:T(8,128)(2,1)S(1)}, u32[]{:S(2)}, u32[]{:S(2)}) collective-permute-start(bf16[1,32,2048]{2,1,0:T(8,128)(2,1)S(1)} %copy.18), channel_id=1, source_target_pairs={{0,1},{1,2},{2,3},{3,4},{4,5},{5,6},{6,7},{7,8},{8,9},{9,10},{10,1... | collective-permute-start | bytes 393224 | tf_op jit(solution)/shard_map/while/body/eval_jaxpr/ppermute | solution.py:14
  213.4 9.0 %collective-permute-start.1 = (bf16[1,32,2048]{2,1,0:T(8,128)(2,1)S(1)}, bf16[1,32,2048]{2,1,0:T(8,128)(2,1)S(1)}, u32[]{:S(2)}, u32[]{:S(2)}) collective-permute-start(bf16[1,32,2048]{2,1,0:T(8,128)(2,1)S(1)} %copy.18), channel_id=1, source_target_pairs={{0,1},{1,2},{2,3},{3,4},{4,5},{5,6},{6,7},{7,8},{8,9},{9,10},{10,1... | collective-permute-start | bytes 393224 | tf_op jit(solution)/shard_map/while/body/eval_jaxpr/ppermute | solution.py:14
  222.4 9.0 %collective-permute-start.1 = (bf16[1,32,2048]{2,1,0:T(8,128)(2,1)S(1)}, bf16[1,32,2048]{2,1,0:T(8,128)(2,1)S(1)}, u32[]{:S(2)}, u32[]{:S(2)}) collective-permute-start(bf16[1,32,2048]{2,1,0:T(8,128)(2,1)S(1)} %copy.18), channel_id=1, source_target_pairs={{0,1},{1,2},{2,3},{3,4},{4,5},{5,6},{6,7},{7,8},{8,9},{9,10},{10,1... | collective-permute-start | bytes 393224 | tf_op jit(solution)/shard_map/while/body/eval_jaxpr/ppermute | solution.py:14
  231.3 10.0 %collective-permute-start.1 = (bf16[1,32,2048]{2,1,0:T(8,128)(2,1)S(1)}, bf16[1,32,2048]{2,1,0:T(8,128)(2,1)S(1)}, u32[]{:S(2)}, u32[]{:S(2)}) collective-permute-start(bf16[1,32,2048]{2,1,0:T(8,128)(2,1)S(1)} %copy.18), channel_id=1, source_target_pairs={{0,1},{1,2},{2,3},{3,4},{4,5},{5,6},{6,7},{7,8},{8,9},{9,10},{10,1... | collective-permute-start | bytes 393224 | tf_op jit(solution)/shard_map/while/body/eval_jaxpr/ppermute | solution.py:14
  241.3 10.1 %collective-permute-start.1 = (bf16[1,32,2048]{2,1,0:T(8,128)(2,1)S(1)}, bf16[1,32,2048]{2,1,0:T(8,128)(2,1)S(1)}, u32[]{:S(2)}, u32[]{:S(2)}) collective-permute-start(bf16[1,32,2048]{2,1,0:T(8,128)(2,1)S(1)} %copy.18), channel_id=1, source_target_pairs={{0,1},{1,2},{2,3},{3,4},{4,5},{5,6},{6,7},{7,8},{8,9},{9,10},{10,1... | collective-permute-start | bytes 393224 | tf_op jit(solution)/shard_map/while/body/eval_jaxpr/ppermute | solution.py:14
  251.4 9.3 %collective-permute-start.1 = (bf16[1,32,2048]{2,1,0:T(8,128)(2,1)S(1)}, bf16[1,32,2048]{2,1,0:T(8,128)(2,1)S(1)}, u32[]{:S(2)}, u32[]{:S(2)}) collective-permute-start(bf16[1,32,2048]{2,1,0:T(8,128)(2,1)S(1)} %copy.18), channel_id=1, source_target_pairs={{0,1},{1,2},{2,3},{3,4},{4,5},{5,6},{6,7},{7,8},{8,9},{9,10},{10,1... | collective-permute-start | bytes 393224 | tf_op jit(solution)/shard_map/while/body/eval_jaxpr/ppermute | solution.py:14
  260.7 9.0 %collective-permute-start.1 = (bf16[1,32,2048]{2,1,0:T(8,128)(2,1)S(1)}, bf16[1,32,2048]{2,1,0:T(8,128)(2,1)S(1)}, u32[]{:S(2)}, u32[]{:S(2)}) collective-permute-start(bf16[1,32,2048]{2,1,0:T(8,128)(2,1)S(1)} %copy.18), channel_id=1, source_target_pairs={{0,1},{1,2},{2,3},{3,4},{4,5},{5,6},{6,7},{7,8},{8,9},{9,10},{10,1... | collective-permute-start | bytes 393224 | tf_op jit(solution)/shard_map/while/body/eval_jaxpr/ppermute | solution.py:14
  269.7 9.0 %collective-permute-start.1 = (bf16[1,32,2048]{2,1,0:T(8,128)(2,1)S(1)}, bf16[1,32,2048]{2,1,0:T(8,128)(2,1)S(1)}, u32[]{:S(2)}, u32[]{:S(2)}) collective-permute-start(bf16[1,32,2048]{2,1,0:T(8,128)(2,1)S(1)} %copy.18), channel_id=1, source_target_pairs={{0,1},{1,2},{2,3},{3,4},{4,5},{5,6},{6,7},{7,8},{8,9},{9,10},{10,1... | collective-permute-start | bytes 393224 | tf_op jit(solution)/shard_map/while/body/eval_jaxpr/ppermute | solution.py:14
  278.7 9.0 %collective-permute-start.1 = (bf16[1,32,2048]{2,1,0:T(8,128)(2,1)S(1)}, bf16[1,32,2048]{2,1,0:T(8,128)(2,1)S(1)}, u32[]{:S(2)}, u32[]{:S(2)}) collective-permute-start(bf16[1,32,2048]{2,1,0:T(8,128)(2,1)S(1)} %copy.18), channel_id=1, source_target_pairs={{0,1},{1,2},{2,3},{3,4},{4,5},{5,6},{6,7},{7,8},{8,9},{9,10},{10,1... | collective-permute-start | bytes 393224 | tf_op jit(solution)/shard_map/while/body/eval_jaxpr/ppermute | solution.py:14
  287.7 9.0 %collective-permute-start.1 = (bf16[1,32,2048]{2,1,0:T(8,128)(2,1)S(1)}, bf16[1,32,2048]{2,1,0:T(8,128)(2,1)S(1)}, u32[]{:S(2)}, u32[]{:S(2)}) collective-permute-start(bf16[1,32,2048]{2,1,0:T(8,128)(2,1)S(1)} %copy.18), channel_id=1, source_target_pairs={{0,1},{1,2},{2,3},{3,4},{4,5},{5,6},{6,7},{7,8},{8,9},{9,10},{10,1... | collective-permute-start | bytes 393224 | tf_op jit(solution)/shard_map/while/body/eval_jaxpr/ppermute | solution.py:14
  296.6 9.1 %collective-permute-start.1 = (bf16[1,32,2048]{2,1,0:T(8,128)(2,1)S(1)}, bf16[1,32,2048]{2,1,0:T(8,128)(2,1)S(1)}, u32[]{:S(2)}, u32[]{:S(2)}) collective-permute-start(bf16[1,32,2048]{2,1,0:T(8,128)(2,1)S(1)} %copy.18), channel_id=1, source_target_pairs={{0,1},{1,2},{2,3},{3,4},{4,5},{5,6},{6,7},{7,8},{8,9},{9,10},{10,1... | collective-permute-start | bytes 393224 | tf_op jit(solution)/shard_map/while/body/eval_jaxpr/ppermute | solution.py:14
  305.8 10.3 %collective-permute-start.1 = (bf16[1,32,2048]{2,1,0:T(8,128)(2,1)S(1)}, bf16[1,32,2048]{2,1,0:T(8,128)(2,1)S(1)}, u32[]{:S(2)}, u32[]{:S(2)}) collective-permute-start(bf16[1,32,2048]{2,1,0:T(8,128)(2,1)S(1)} %copy.18), channel_id=1, source_target_pairs={{0,1},{1,2},{2,3},{3,4},{4,5},{5,6},{6,7},{7,8},{8,9},{9,10},{10,1... | collective-permute-start | bytes 393224 | tf_op jit(solution)/shard_map/while/body/eval_jaxpr/ppermute | solution.py:14
  316.0 9.5 %collective-permute-start.1 = (bf16[1,32,2048]{2,1,0:T(8,128)(2,1)S(1)}, bf16[1,32,2048]{2,1,0:T(8,128)(2,1)S(1)}, u32[]{:S(2)}, u32[]{:S(2)}) collective-permute-start(bf16[1,32,2048]{2,1,0:T(8,128)(2,1)S(1)} %copy.18), channel_id=1, source_target_pairs={{0,1},{1,2},{2,3},{3,4},{4,5},{5,6},{6,7},{7,8},{8,9},{9,10},{10,1... | collective-permute-start | bytes 393224 | tf_op jit(solution)/shard_map/while/body/eval_jaxpr/ppermute | solution.py:14
  325.6 9.0 %collective-permute-start.1 = (bf16[1,32,2048]{2,1,0:T(8,128)(2,1)S(1)}, bf16[1,32,2048]{2,1,0:T(8,128)(2,1)S(1)}, u32[]{:S(2)}, u32[]{:S(2)}) collective-permute-start(bf16[1,32,2048]{2,1,0:T(8,128)(2,1)S(1)} %copy.18), channel_id=1, source_target_pairs={{0,1},{1,2},{2,3},{3,4},{4,5},{5,6},{6,7},{7,8},{8,9},{9,10},{10,1... | collective-permute-start | bytes 393224 | tf_op jit(solution)/shard_map/while/body/eval_jaxpr/ppermute | solution.py:14
  334.6 9.0 %collective-permute-start.1 = (bf16[1,32,2048]{2,1,0:T(8,128)(2,1)S(1)}, bf16[1,32,2048]{2,1,0:T(8,128)(2,1)S(1)}, u32[]{:S(2)}, u32[]{:S(2)}) collective-permute-start(bf16[1,32,2048]{2,1,0:T(8,128)(2,1)S(1)} %copy.18), channel_id=1, source_target_pairs={{0,1},{1,2},{2,3},{3,4},{4,5},{5,6},{6,7},{7,8},{8,9},{9,10},{10,1... | collective-permute-start | bytes 393224 | tf_op jit(solution)/shard_map/while/body/eval_jaxpr/ppermute | solution.py:14
  343.6 9.0 %collective-permute-start.1 = (bf16[1,32,2048]{2,1,0:T(8,128)(2,1)S(1)}, bf16[1,32,2048]{2,1,0:T(8,128)(2,1)S(1)}, u32[]{:S(2)}, u32[]{:S(2)}) collective-permute-start(bf16[1,32,2048]{2,1,0:T(8,128)(2,1)S(1)} %copy.18), channel_id=1, source_target_pairs={{0,1},{1,2},{2,3},{3,4},{4,5},{5,6},{6,7},{7,8},{8,9},{9,10},{10,1... | collective-permute-start | bytes 393224 | tf_op jit(solution)/shard_map/while/body/eval_jaxpr/ppermute | solution.py:14
  352.5 9.0 %collective-permute-start.1 = (bf16[1,32,2048]{2,1,0:T(8,128)(2,1)S(1)}, bf16[1,32,2048]{2,1,0:T(8,128)(2,1)S(1)}, u32[]{:S(2)}, u32[]{:S(2)}) collective-permute-start(bf16[1,32,2048]{2,1,0:T(8,128)(2,1)S(1)} %copy.18), channel_id=1, source_target_pairs={{0,1},{1,2},{2,3},{3,4},{4,5},{5,6},{6,7},{7,8},{8,9},{9,10},{10,1... | collective-permute-start | bytes 393224 | tf_op jit(solution)/shard_map/while/body/eval_jaxpr/ppermute | solution.py:14
  361.5 9.0 %collective-permute-start.1 = (bf16[1,32,2048]{2,1,0:T(8,128)(2,1)S(1)}, bf16[1,32,2048]{2,1,0:T(8,128)(2,1)S(1)}, u32[]{:S(2)}, u32[]{:S(2)}) collective-permute-start(bf16[1,32,2048]{2,1,0:T(8,128)(2,1)S(1)} %copy.18), channel_id=1, source_target_pairs={{0,1},{1,2},{2,3},{3,4},{4,5},{5,6},{6,7},{7,8},{8,9},{9,10},{10,1... | collective-permute-start | bytes 393224 | tf_op jit(solution)/shard_map/while/body/eval_jaxpr/ppermute | solution.py:14
  370.5 10.0 %collective-permute-start.1 = (bf16[1,32,2048]{2,1,0:T(8,128)(2,1)S(1)}, bf16[1,32,2048]{2,1,0:T(8,128)(2,1)S(1)}, u32[]{:S(2)}, u32[]{:S(2)}) collective-permute-start(bf16[1,32,2048]{2,1,0:T(8,128)(2,1)S(1)} %copy.18), channel_id=1, source_target_pairs={{0,1},{1,2},{2,3},{3,4},{4,5},{5,6},{6,7},{7,8},{8,9},{9,10},{10,1... | collective-permute-start | bytes 393224 | tf_op jit(solution)/shard_map/while/body/eval_jaxpr/ppermute | solution.py:14
  380.5 9.6 %collective-permute-start.1 = (bf16[1,32,2048]{2,1,0:T(8,128)(2,1)S(1)}, bf16[1,32,2048]{2,1,0:T(8,128)(2,1)S(1)}, u32[]{:S(2)}, u32[]{:S(2)}) collective-permute-start(bf16[1,32,2048]{2,1,0:T(8,128)(2,1)S(1)} %copy.18), channel_id=1, source_target_pairs={{0,1},{1,2},{2,3},{3,4},{4,5},{5,6},{6,7},{7,8},{8,9},{9,10},{10,1... | collective-permute-start | bytes 393224 | tf_op jit(solution)/shard_map/while/body/eval_jaxpr/ppermute | solution.py:14
  390.1 9.0 %collective-permute-start.1 = (bf16[1,32,2048]{2,1,0:T(8,128)(2,1)S(1)}, bf16[1,32,2048]{2,1,0:T(8,128)(2,1)S(1)}, u32[]{:S(2)}, u32[]{:S(2)}) collective-permute-start(bf16[1,32,2048]{2,1,0:T(8,128)(2,1)S(1)} %copy.18), channel_id=1, source_target_pairs={{0,1},{1,2},{2,3},{3,4},{4,5},{5,6},{6,7},{7,8},{8,9},{9,10},{10,1... | collective-permute-start | bytes 393224 | tf_op jit(solution)/shard_map/while/body/eval_jaxpr/ppermute | solution.py:14
  399.1 9.0 %collective-permute-start.1 = (bf16[1,32,2048]{2,1,0:T(8,128)(2,1)S(1)}, bf16[1,32,2048]{2,1,0:T(8,128)(2,1)S(1)}, u32[]{:S(2)}, u32[]{:S(2)}) collective-permute-start(bf16[1,32,2048]{2,1,0:T(8,128)(2,1)S(1)} %copy.18), channel_id=1, source_target_pairs={{0,1},{1,2},{2,3},{3,4},{4,5},{5,6},{6,7},{7,8},{8,9},{9,10},{10,1... | collective-permute-start | bytes 393224 | tf_op jit(solution)/shard_map/while/body/eval_jaxpr/ppermute | solution.py:14
  408.1 9.0 %collective-permute-start.1 = (bf16[1,32,2048]{2,1,0:T(8,128)(2,1)S(1)}, bf16[1,32,2048]{2,1,0:T(8,128)(2,1)S(1)}, u32[]{:S(2)}, u32[]{:S(2)}) collective-permute-start(bf16[1,32,2048]{2,1,0:T(8,128)(2,1)S(1)} %copy.18), channel_id=1, source_target_pairs={{0,1},{1,2},{2,3},{3,4},{4,5},{5,6},{6,7},{7,8},{8,9},{9,10},{10,1... | collective-permute-start | bytes 393224 | tf_op jit(solution)/shard_map/while/body/eval_jaxpr/ppermute | solution.py:14
  417.1 9.0 %collective-permute-start.1 = (bf16[1,32,2048]{2,1,0:T(8,128)(2,1)S(1)}, bf16[1,32,2048]{2,1,0:T(8,128)(2,1)S(1)}, u32[]{:S(2)}, u32[]{:S(2)}) collective-permute-start(bf16[1,32,2048]{2,1,0:T(8,128)(2,1)S(1)} %copy.18), channel_id=1, source_target_pairs={{0,1},{1,2},{2,3},{3,4},{4,5},{5,6},{6,7},{7,8},{8,9},{9,10},{10,1... | collective-permute-start | bytes 393224 | tf_op jit(solution)/shard_map/while/body/eval_jaxpr/ppermute | solution.py:14
  426.1 9.0 %collective-permute-start.1 = (bf16[1,32,2048]{2,1,0:T(8,128)(2,1)S(1)}, bf16[1,32,2048]{2,1,0:T(8,128)(2,1)S(1)}, u32[]{:S(2)}, u32[]{:S(2)}) collective-permute-start(bf16[1,32,2048]{2,1,0:T(8,128)(2,1)S(1)} %copy.18), channel_id=1, source_target_pairs={{0,1},{1,2},{2,3},{3,4},{4,5},{5,6},{6,7},{7,8},{8,9},{9,10},{10,1... | collective-permute-start | bytes 393224 | tf_op jit(solution)/shard_map/while/body/eval_jaxpr/ppermute | solution.py:14
  435.1 9.0 %collective-permute-start.1 = (bf16[1,32,2048]{2,1,0:T(8,128)(2,1)S(1)}, bf16[1,32,2048]{2,1,0:T(8,128)(2,1)S(1)}, u32[]{:S(2)}, u32[]{:S(2)}) collective-permute-start(bf16[1,32,2048]{2,1,0:T(8,128)(2,1)S(1)} %copy.18), channel_id=1, source_target_pairs={{0,1},{1,2},{2,3},{3,4},{4,5},{5,6},{6,7},{7,8},{8,9},{9,10},{10,1... | collective-permute-start | bytes 393224 | tf_op jit(solution)/shard_map/while/body/eval_jaxpr/ppermute | solution.py:14
  444.0 9.0 %collective-permute-start.1 = (bf16[1,32,2048]{2,1,0:T(8,128)(2,1)S(1)}, bf16[1,32,2048]{2,1,0:T(8,128)(2,1)S(1)}, u32[]{:S(2)}, u32[]{:S(2)}) collective-permute-start(bf16[1,32,2048]{2,1,0:T(8,128)(2,1)S(1)} %copy.18), channel_id=1, source_target_pairs={{0,1},{1,2},{2,3},{3,4},{4,5},{5,6},{6,7},{7,8},{8,9},{9,10},{10,1... | collective-permute-start | bytes 393224 | tf_op jit(solution)/shard_map/while/body/eval_jaxpr/ppermute | solution.py:14
  453.0 9.0 %collective-permute-start.1 = (bf16[1,32,2048]{2,1,0:T(8,128)(2,1)S(1)}, bf16[1,32,2048]{2,1,0:T(8,128)(2,1)S(1)}, u32[]{:S(2)}, u32[]{:S(2)}) collective-permute-start(bf16[1,32,2048]{2,1,0:T(8,128)(2,1)S(1)} %copy.18), channel_id=1, source_target_pairs={{0,1},{1,2},{2,3},{3,4},{4,5},{5,6},{6,7},{7,8},{8,9},{9,10},{10,1... | collective-permute-start | bytes 393224 | tf_op jit(solution)/shard_map/while/body/eval_jaxpr/ppermute | solution.py:14
  467.1 9.0 %collective-permute-start = (bf16[1,32,2048]{2,1,0:T(8,128)(2,1)S(1)}, bf16[1,32,2048]{2,1,0:T(8,128)(2,1)S(1)}, u32[]{:S(2)}, u32[]{:S(2)}) collective-permute-start(bf16[1,32,2048]{2,1,0:T(8,128)(2,1)S(1)} %copy.30), channel_id=1, source_target_pairs={{0,1},{1,2},{2,3},{3,4},{4,5},{5,6},{6,7},{7,8},{8,9},{9,10},{10,1... | collective-permute-start | bytes 393224 | tf_op jit(solution)/shard_map/while/body/eval_jaxpr/ppermute | solution.py:14
  476.1 9.0 %collective-permute-start = (bf16[1,32,2048]{2,1,0:T(8,128)(2,1)S(1)}, bf16[1,32,2048]{2,1,0:T(8,128)(2,1)S(1)}, u32[]{:S(2)}, u32[]{:S(2)}) collective-permute-start(bf16[1,32,2048]{2,1,0:T(8,128)(2,1)S(1)} %copy.30), channel_id=1, source_target_pairs={{0,1},{1,2},{2,3},{3,4},{4,5},{5,6},{6,7},{7,8},{8,9},{9,10},{10,1... | collective-permute-start | bytes 393224 | tf_op jit(solution)/shard_map/while/body/eval_jaxpr/ppermute | solution.py:14
  485.1 9.0 %collective-permute-start = (bf16[1,32,2048]{2,1,0:T(8,128)(2,1)S(1)}, bf16[1,32,2048]{2,1,0:T(8,128)(2,1)S(1)}, u32[]{:S(2)}, u32[]{:S(2)}) collective-permute-start(bf16[1,32,2048]{2,1,0:T(8,128)(2,1)S(1)} %copy.30), channel_id=1, source_target_pairs={{0,1},{1,2},{2,3},{3,4},{4,5},{5,6},{6,7},{7,8},{8,9},{9,10},{10,1... | collective-permute-start | bytes 393224 | tf_op jit(solution)/shard_map/while/body/eval_jaxpr/ppermute | solution.py:14
  494.1 9.0 %collective-permute-start = (bf16[1,32,2048]{2,1,0:T(8,128)(2,1)S(1)}, bf16[1,32,2048]{2,1,0:T(8,128)(2,1)S(1)}, u32[]{:S(2)}, u32[]{:S(2)}) collective-permute-start(bf16[1,32,2048]{2,1,0:T(8,128)(2,1)S(1)} %copy.30), channel_id=1, source_target_pairs={{0,1},{1,2},{2,3},{3,4},{4,5},{5,6},{6,7},{7,8},{8,9},{9,10},{10,1... | collective-permute-start | bytes 393224 | tf_op jit(solution)/shard_map/while/body/eval_jaxpr/ppermute | solution.py:14
  503.1 10.1 %collective-permute-start = (bf16[1,32,2048]{2,1,0:T(8,128)(2,1)S(1)}, bf16[1,32,2048]{2,1,0:T(8,128)(2,1)S(1)}, u32[]{:S(2)}, u32[]{:S(2)}) collective-permute-start(bf16[1,32,2048]{2,1,0:T(8,128)(2,1)S(1)} %copy.30), channel_id=1, source_target_pairs={{0,1},{1,2},{2,3},{3,4},{4,5},{5,6},{6,7},{7,8},{8,9},{9,10},{10,1... | collective-permute-start | bytes 393224 | tf_op jit(solution)/shard_map/while/body/eval_jaxpr/ppermute | solution.py:14
  513.2 9.5 %collective-permute-start = (bf16[1,32,2048]{2,1,0:T(8,128)(2,1)S(1)}, bf16[1,32,2048]{2,1,0:T(8,128)(2,1)S(1)}, u32[]{:S(2)}, u32[]{:S(2)}) collective-permute-start(bf16[1,32,2048]{2,1,0:T(8,128)(2,1)S(1)} %copy.30), channel_id=1, source_target_pairs={{0,1},{1,2},{2,3},{3,4},{4,5},{5,6},{6,7},{7,8},{8,9},{9,10},{10,1... | collective-permute-start | bytes 393224 | tf_op jit(solution)/shard_map/while/body/eval_jaxpr/ppermute | solution.py:14
  522.7 9.0 %collective-permute-start = (bf16[1,32,2048]{2,1,0:T(8,128)(2,1)S(1)}, bf16[1,32,2048]{2,1,0:T(8,128)(2,1)S(1)}, u32[]{:S(2)}, u32[]{:S(2)}) collective-permute-start(bf16[1,32,2048]{2,1,0:T(8,128)(2,1)S(1)} %copy.30), channel_id=1, source_target_pairs={{0,1},{1,2},{2,3},{3,4},{4,5},{5,6},{6,7},{7,8},{8,9},{9,10},{10,1... | collective-permute-start | bytes 393224 | tf_op jit(solution)/shard_map/while/body/eval_jaxpr/ppermute | solution.py:14
  531.7 9.0 %collective-permute-start = (bf16[1,32,2048]{2,1,0:T(8,128)(2,1)S(1)}, bf16[1,32,2048]{2,1,0:T(8,128)(2,1)S(1)}, u32[]{:S(2)}, u32[]{:S(2)}) collective-permute-start(bf16[1,32,2048]{2,1,0:T(8,128)(2,1)S(1)} %copy.30), channel_id=1, source_target_pairs={{0,1},{1,2},{2,3},{3,4},{4,5},{5,6},{6,7},{7,8},{8,9},{9,10},{10,1... | collective-permute-start | bytes 393224 | tf_op jit(solution)/shard_map/while/body/eval_jaxpr/ppermute | solution.py:14
  540.7 9.0 %collective-permute-start = (bf16[1,32,2048]{2,1,0:T(8,128)(2,1)S(1)}, bf16[1,32,2048]{2,1,0:T(8,128)(2,1)S(1)}, u32[]{:S(2)}, u32[]{:S(2)}) collective-permute-start(bf16[1,32,2048]{2,1,0:T(8,128)(2,1)S(1)} %copy.30), channel_id=1, source_target_pairs={{0,1},{1,2},{2,3},{3,4},{4,5},{5,6},{6,7},{7,8},{8,9},{9,10},{10,1... | collective-permute-start | bytes 393224 | tf_op jit(solution)/shard_map/while/body/eval_jaxpr/ppermute | solution.py:14
  549.7 9.0 %collective-permute-start = (bf16[1,32,2048]{2,1,0:T(8,128)(2,1)S(1)}, bf16[1,32,2048]{2,1,0:T(8,128)(2,1)S(1)}, u32[]{:S(2)}, u32[]{:S(2)}) collective-permute-start(bf16[1,32,2048]{2,1,0:T(8,128)(2,1)S(1)} %copy.30), channel_id=1, source_target_pairs={{0,1},{1,2},{2,3},{3,4},{4,5},{5,6},{6,7},{7,8},{8,9},{9,10},{10,1... | collective-permute-start | bytes 393224 | tf_op jit(solution)/shard_map/while/body/eval_jaxpr/ppermute | solution.py:14
  558.7 9.0 %collective-permute-start = (bf16[1,32,2048]{2,1,0:T(8,128)(2,1)S(1)}, bf16[1,32,2048]{2,1,0:T(8,128)(2,1)S(1)}, u32[]{:S(2)}, u32[]{:S(2)}) collective-permute-start(bf16[1,32,2048]{2,1,0:T(8,128)(2,1)S(1)} %copy.30), channel_id=1, source_target_pairs={{0,1},{1,2},{2,3},{3,4},{4,5},{5,6},{6,7},{7,8},{8,9},{9,10},{10,1... | collective-permute-start | bytes 393224 | tf_op jit(solution)/shard_map/while/body/eval_jaxpr/ppermute | solution.py:14
  567.6 10.0 %collective-permute-start = (bf16[1,32,2048]{2,1,0:T(8,128)(2,1)S(1)}, bf16[1,32,2048]{2,1,0:T(8,128)(2,1)S(1)}, u32[]{:S(2)}, u32[]{:S(2)}) collective-permute-start(bf16[1,32,2048]{2,1,0:T(8,128)(2,1)S(1)} %copy.30), channel_id=1, source_target_pairs={{0,1},{1,2},{2,3},{3,4},{4,5},{5,6},{6,7},{7,8},{8,9},{9,10},{10,1... | collective-permute-start | bytes 393224 | tf_op jit(solution)/shard_map/while/body/eval_jaxpr/ppermute | solution.py:14
  577.7 9.6 %collective-permute-start = (bf16[1,32,2048]{2,1,0:T(8,128)(2,1)S(1)}, bf16[1,32,2048]{2,1,0:T(8,128)(2,1)S(1)}, u32[]{:S(2)}, u32[]{:S(2)}) collective-permute-start(bf16[1,32,2048]{2,1,0:T(8,128)(2,1)S(1)} %copy.30), channel_id=1, source_target_pairs={{0,1},{1,2},{2,3},{3,4},{4,5},{5,6},{6,7},{7,8},{8,9},{9,10},{10,1... | collective-permute-start | bytes 393224 | tf_op jit(solution)/shard_map/while/body/eval_jaxpr/ppermute | solution.py:14
  587.3 9.0 %collective-permute-start = (bf16[1,32,2048]{2,1,0:T(8,128)(2,1)S(1)}, bf16[1,32,2048]{2,1,0:T(8,128)(2,1)S(1)}, u32[]{:S(2)}, u32[]{:S(2)}) collective-permute-start(bf16[1,32,2048]{2,1,0:T(8,128)(2,1)S(1)} %copy.30), channel_id=1, source_target_pairs={{0,1},{1,2},{2,3},{3,4},{4,5},{5,6},{6,7},{7,8},{8,9},{9,10},{10,1... | collective-permute-start | bytes 393224 | tf_op jit(solution)/shard_map/while/body/eval_jaxpr/ppermute | solution.py:14
  596.3 9.0 %collective-permute-start = (bf16[1,32,2048]{2,1,0:T(8,128)(2,1)S(1)}, bf16[1,32,2048]{2,1,0:T(8,128)(2,1)S(1)}, u32[]{:S(2)}, u32[]{:S(2)}) collective-permute-start(bf16[1,32,2048]{2,1,0:T(8,128)(2,1)S(1)} %copy.30), channel_id=1, source_target_pairs={{0,1},{1,2},{2,3},{3,4},{4,5},{5,6},{6,7},{7,8},{8,9},{9,10},{10,1... | collective-permute-start | bytes 393224 | tf_op jit(solution)/shard_map/while/body/eval_jaxpr/ppermute | solution.py:14
  605.2 9.0 %collective-permute-start = (bf16[1,32,2048]{2,1,0:T(8,128)(2,1)S(1)}, bf16[1,32,2048]{2,1,0:T(8,128)(2,1)S(1)}, u32[]{:S(2)}, u32[]{:S(2)}) collective-permute-start(bf16[1,32,2048]{2,1,0:T(8,128)(2,1)S(1)} %copy.30), channel_id=1, source_target_pairs={{0,1},{1,2},{2,3},{3,4},{4,5},{5,6},{6,7},{7,8},{8,9},{9,10},{10,1... | collective-permute-start | bytes 393224 | tf_op jit(solution)/shard_map/while/body/eval_jaxpr/ppermute | solution.py:14
  614.2 9.0 %collective-permute-start = (bf16[1,32,2048]{2,1,0:T(8,128)(2,1)S(1)}, bf16[1,32,2048]{2,1,0:T(8,128)(2,1)S(1)}, u32[]{:S(2)}, u32[]{:S(2)}) collective-permute-start(bf16[1,32,2048]{2,1,0:T(8,128)(2,1)S(1)} %copy.30), channel_id=1, source_target_pairs={{0,1},{1,2},{2,3},{3,4},{4,5},{5,6},{6,7},{7,8},{8,9},{9,10},{10,1... | collective-permute-start | bytes 393224 | tf_op jit(solution)/shard_map/while/body/eval_jaxpr/ppermute | solution.py:14
  623.2 9.0 %collective-permute-start = (bf16[1,32,2048]{2,1,0:T(8,128)(2,1)S(1)}, bf16[1,32,2048]{2,1,0:T(8,128)(2,1)S(1)}, u32[]{:S(2)}, u32[]{:S(2)}) collective-permute-start(bf16[1,32,2048]{2,1,0:T(8,128)(2,1)S(1)} %copy.30), channel_id=1, source_target_pairs={{0,1},{1,2},{2,3},{3,4},{4,5},{5,6},{6,7},{7,8},{8,9},{9,10},{10,1... | collective-permute-start | bytes 393224 | tf_op jit(solution)/shard_map/while/body/eval_jaxpr/ppermute | solution.py:14
  632.2 9.9 %collective-permute-start = (bf16[1,32,2048]{2,1,0:T(8,128)(2,1)S(1)}, bf16[1,32,2048]{2,1,0:T(8,128)(2,1)S(1)}, u32[]{:S(2)}, u32[]{:S(2)}) collective-permute-start(bf16[1,32,2048]{2,1,0:T(8,128)(2,1)S(1)} %copy.30), channel_id=1, source_target_pairs={{0,1},{1,2},{2,3},{3,4},{4,5},{5,6},{6,7},{7,8},{8,9},{9,10},{10,1... | collective-permute-start | bytes 393224 | tf_op jit(solution)/shard_map/while/body/eval_jaxpr/ppermute | solution.py:14
  642.1 9.7 %collective-permute-start = (bf16[1,32,2048]{2,1,0:T(8,128)(2,1)S(1)}, bf16[1,32,2048]{2,1,0:T(8,128)(2,1)S(1)}, u32[]{:S(2)}, u32[]{:S(2)}) collective-permute-start(bf16[1,32,2048]{2,1,0:T(8,128)(2,1)S(1)} %copy.30), channel_id=1, source_target_pairs={{0,1},{1,2},{2,3},{3,4},{4,5},{5,6},{6,7},{7,8},{8,9},{9,10},{10,1... | collective-permute-start | bytes 393224 | tf_op jit(solution)/shard_map/while/body/eval_jaxpr/ppermute | solution.py:14
  651.8 9.0 %collective-permute-start = (bf16[1,32,2048]{2,1,0:T(8,128)(2,1)S(1)}, bf16[1,32,2048]{2,1,0:T(8,128)(2,1)S(1)}, u32[]{:S(2)}, u32[]{:S(2)}) collective-permute-start(bf16[1,32,2048]{2,1,0:T(8,128)(2,1)S(1)} %copy.30), channel_id=1, source_target_pairs={{0,1},{1,2},{2,3},{3,4},{4,5},{5,6},{6,7},{7,8},{8,9},{9,10},{10,1... | collective-permute-start | bytes 393224 | tf_op jit(solution)/shard_map/while/body/eval_jaxpr/ppermute | solution.py:14
  660.8 9.0 %collective-permute-start = (bf16[1,32,2048]{2,1,0:T(8,128)(2,1)S(1)}, bf16[1,32,2048]{2,1,0:T(8,128)(2,1)S(1)}, u32[]{:S(2)}, u32[]{:S(2)}) collective-permute-start(bf16[1,32,2048]{2,1,0:T(8,128)(2,1)S(1)} %copy.30), channel_id=1, source_target_pairs={{0,1},{1,2},{2,3},{3,4},{4,5},{5,6},{6,7},{7,8},{8,9},{9,10},{10,1... | collective-permute-start | bytes 393224 | tf_op jit(solution)/shard_map/while/body/eval_jaxpr/ppermute | solution.py:14
  669.8 9.0 %collective-permute-start = (bf16[1,32,2048]{2,1,0:T(8,128)(2,1)S(1)}, bf16[1,32,2048]{2,1,0:T(8,128)(2,1)S(1)}, u32[]{:S(2)}, u32[]{:S(2)}) collective-permute-start(bf16[1,32,2048]{2,1,0:T(8,128)(2,1)S(1)} %copy.30), channel_id=1, source_target_pairs={{0,1},{1,2},{2,3},{3,4},{4,5},{5,6},{6,7},{7,8},{8,9},{9,10},{10,1... | collective-permute-start | bytes 393224 | tf_op jit(solution)/shard_map/while/body/eval_jaxpr/ppermute | solution.py:14
  678.8 9.0 %collective-permute-start = (bf16[1,32,2048]{2,1,0:T(8,128)(2,1)S(1)}, bf16[1,32,2048]{2,1,0:T(8,128)(2,1)S(1)}, u32[]{:S(2)}, u32[]{:S(2)}) collective-permute-start(bf16[1,32,2048]{2,1,0:T(8,128)(2,1)S(1)} %copy.30), channel_id=1, source_target_pairs={{0,1},{1,2},{2,3},{3,4},{4,5},{5,6},{6,7},{7,8},{8,9},{9,10},{10,1... | collective-permute-start | bytes 393224 | tf_op jit(solution)/shard_map/while/body/eval_jaxpr/ppermute | solution.py:14
  687.8 9.0 %collective-permute-start = (bf16[1,32,2048]{2,1,0:T(8,128)(2,1)S(1)}, bf16[1,32,2048]{2,1,0:T(8,128)(2,1)S(1)}, u32[]{:S(2)}, u32[]{:S(2)}) collective-permute-start(bf16[1,32,2048]{2,1,0:T(8,128)(2,1)S(1)} %copy.30), channel_id=1, source_target_pairs={{0,1},{1,2},{2,3},{3,4},{4,5},{5,6},{6,7},{7,8},{8,9},{9,10},{10,1... | collective-permute-start | bytes 393224 | tf_op jit(solution)/shard_map/while/body/eval_jaxpr/ppermute | solution.py:14
  696.8 9.0 %collective-permute-start = (bf16[1,32,2048]{2,1,0:T(8,128)(2,1)S(1)}, bf16[1,32,2048]{2,1,0:T(8,128)(2,1)S(1)}, u32[]{:S(2)}, u32[]{:S(2)}) collective-permute-start(bf16[1,32,2048]{2,1,0:T(8,128)(2,1)S(1)} %copy.30), channel_id=1, source_target_pairs={{0,1},{1,2},{2,3},{3,4},{4,5},{5,6},{6,7},{7,8},{8,9},{9,10},{10,1... | collective-permute-start | bytes 393224 | tf_op jit(solution)/shard_map/while/body/eval_jaxpr/ppermute | solution.py:14
  705.7 9.0 %collective-permute-start = (bf16[1,32,2048]{2,1,0:T(8,128)(2,1)S(1)}, bf16[1,32,2048]{2,1,0:T(8,128)(2,1)S(1)}, u32[]{:S(2)}, u32[]{:S(2)}) collective-permute-start(bf16[1,32,2048]{2,1,0:T(8,128)(2,1)S(1)} %copy.30), channel_id=1, source_target_pairs={{0,1},{1,2},{2,3},{3,4},{4,5},{5,6},{6,7},{7,8},{8,9},{9,10},{10,1... | collective-permute-start | bytes 393224 | tf_op jit(solution)/shard_map/while/body/eval_jaxpr/ppermute | solution.py:14
  714.7 9.0 %collective-permute-start = (bf16[1,32,2048]{2,1,0:T(8,128)(2,1)S(1)}, bf16[1,32,2048]{2,1,0:T(8,128)(2,1)S(1)}, u32[]{:S(2)}, u32[]{:S(2)}) collective-permute-start(bf16[1,32,2048]{2,1,0:T(8,128)(2,1)S(1)} %copy.30), channel_id=1, source_target_pairs={{0,1},{1,2},{2,3},{3,4},{4,5},{5,6},{6,7},{7,8},{8,9},{9,10},{10,1... | collective-permute-start | bytes 393224 | tf_op jit(solution)/shard_map/while/body/eval_jaxpr/ppermute | solution.py:14
  723.7 9.0 %collective-permute-start = (bf16[1,32,2048]{2,1,0:T(8,128)(2,1)S(1)}, bf16[1,32,2048]{2,1,0:T(8,128)(2,1)S(1)}, u32[]{:S(2)}, u32[]{:S(2)}) collective-permute-start(bf16[1,32,2048]{2,1,0:T(8,128)(2,1)S(1)} %copy.30), channel_id=1, source_target_pairs={{0,1},{1,2},{2,3},{3,4},{4,5},{5,6},{6,7},{7,8},{8,9},{9,10},{10,1... | collective-permute-start | bytes 393224 | tf_op jit(solution)/shard_map/while/body/eval_jaxpr/ppermute | solution.py:14
  732.7 9.0 %collective-permute-start = (bf16[1,32,2048]{2,1,0:T(8,128)(2,1)S(1)}, bf16[1,32,2048]{2,1,0:T(8,128)(2,1)S(1)}, u32[]{:S(2)}, u32[]{:S(2)}) collective-permute-start(bf16[1,32,2048]{2,1,0:T(8,128)(2,1)S(1)} %copy.30), channel_id=1, source_target_pairs={{0,1},{1,2},{2,3},{3,4},{4,5},{5,6},{6,7},{7,8},{8,9},{9,10},{10,1... | collective-permute-start | bytes 393224 | tf_op jit(solution)/shard_map/while/body/eval_jaxpr/ppermute | solution.py:14
  741.7 9.0 %collective-permute-start = (bf16[1,32,2048]{2,1,0:T(8,128)(2,1)S(1)}, bf16[1,32,2048]{2,1,0:T(8,128)(2,1)S(1)}, u32[]{:S(2)}, u32[]{:S(2)}) collective-permute-start(bf16[1,32,2048]{2,1,0:T(8,128)(2,1)S(1)} %copy.30), channel_id=1, source_target_pairs={{0,1},{1,2},{2,3},{3,4},{4,5},{5,6},{6,7},{7,8},{8,9},{9,10},{10,1... | collective-permute-start | bytes 393224 | tf_op jit(solution)/shard_map/while/body/eval_jaxpr/ppermute | solution.py:14
  750.6 5.5 copy-start.4
  (4 other events, 12.6 us)
Sparse Core Ops, SparseCore 0:
  13.7 158.4 all-reduce.2
where the time goes:
time: 779 us; the launch traced here: 775 us
  waiting for transfers between devices  337 us (43%)
  local copies, waits for them, and re-layouts  246 us (32%)
  starting transfers between devices  121 us (16%)
  matrix products  45.6 us (6%)
  between operations  17.4 us (2%)
    dynamic_update_slice x64, local copies, waits for them, and re-layouts, place(): scores = lax.dynamic_update_slice_in_dim(scores, columns, offset, 3)  192 us
    ppermute x62, waiting for transfers between devices, passed_along(): lax.ppermute(shard, axis, [(i, (i + by) % count) for i in range(count)])  184 us
    psum x1, waiting for transfers between devices, broadcast(): return lax.psum(kept, axis)  154 us
    ppermute x62, starting transfers between devices, passed_along(): lax.ppermute(shard, axis, [(i, (i + by) % count) for i in range(count)])  121 us
    dynamic_update_slice x63, local copies, waits for them, and re-layouts, place(): lax.dynamic_update_slice_in_dim(whole_block, piece_rows, offset, 1)  41.6 us
    dot_general x64, matrix products, place(): jnp.einsum('iap,srp->siar', integrals, piece_rows, preferred_element_type...  36.5 us
  transfers between devices with their start and end apart: 63, of which 63 were waited for; matrix products, arithmetic and copies ran while one was open for 34% of the time, Pallas kernels for 0%

commit v1 on v0

v1 whole, which is shorter than its diff:
```python
import jax
import jax.numpy as jnp
from jax import lax
from jax.experimental import pallas as pl
from jax.experimental.pallas import tpu as pltpu
from jax.sharding import PartitionSpec as P

MESH = pl.DeviceIdType.MESH
BF16, F32 = jnp.bfloat16, jnp.float32
NX, NY, NC, NZ = 4, 4, 2, 16
NOCC_AX = 16
LANES = 128
PAIRS = NZ // 2
STAGES = 5


def kernel(
    partners, occ_energy, virt_energy, x_hbm, out_hbm,
    xv, pieces, got, ybuf, acc, outv, va, own, vb,
    x_sem, out_sem, rs_send, rs_recv, z_send, z_recv,
    a_send, a_recv, b_send, b_recv, c_send, c_recv,
):
    occ_dev, local_virt, aux = xv.shape
    rows = occ_dev * local_virt
    o, v = lax.axis_index("occ"), lax.axis_index("virt")
    x, yh, c = o // 4, (o // 2) % 2, o % 2
    yl, z = v // NZ, v % NZ
    y = 2 * yh + yl
    step_dir = 1 - 2 * c

    def at(xx, yy, cc, zz):
        return {"occ": (xx * 2 + yy // 2) * 2 + cc, "virt": (yy % 2) * NZ + zz}

    def send(src, dst, s_sem, r_sem, device):
        return pltpu.make_async_remote_copy(
            src_ref=src, dst_ref=dst, send_sem=s_sem, recv_sem=r_sem,
            device_id=device, device_id_type=MESH,
        )

    def x_at(d):
        return at((x + d + NX) % NX, y, c, z)

    def y_at(d):
        return at(x, (y + d + NY) % NY, c, z)

    def occ_at(j):
        return {"occ": (o + j) % NOCC_AX, "virt": v}

    def z_at(d):
        return at(x, y, c, (z + d + NZ) % NZ)

    barrier = pltpu.get_barrier_semaphore()
    peers = [occ_at(j) for j in range(1, NOCC_AX)]
    peers += [y_at(1), y_at(-1)]
    peers += [z_at(j) for j in range(1, NZ)]
    for peer in peers:
        pl.semaphore_signal(barrier, inc=1, device_id=peer, device_id_type=MESH)

    x_copy = pltpu.make_async_copy(x_hbm, xv, x_sem)
    x_copy.start()

    lane = lax.broadcasted_iota(jnp.int32, (local_virt, LANES), 1)
    sub = lax.broadcasted_iota(jnp.int32, (local_virt, LANES), 0)
    line = jnp.broadcast_to(virt_energy[pl.ds(v // 4, 1), :], (local_virt, LANES))
    mine = jnp.sum(jnp.where(lane == sub + (v % 4) * local_virt, line, 0.0), axis=1, keepdims=True)
    mine = jnp.broadcast_to(mine, (local_virt, LANES))
    for i in range(occ_dev):
        va[pl.ds(i * local_virt, local_virt), :] = mine
        own[pl.ds(i * local_virt, local_virt), :] = jnp.full((local_virt, LANES), occ_energy[o * occ_dev + i], F32)
    lane8 = lax.broadcasted_iota(jnp.int32, (8, LANES), 1)
    for k in range(PAIRS):
        total = jnp.zeros((8, LANES), F32)
        for yy in range(2):
            for sign in range(2):
                zz = (z + NZ - k) % NZ if sign == 0 else (z + k + 1) % NZ
                row = jnp.broadcast_to(virt_energy[pl.ds(yy * 4 + zz // 4, 1), :], (8, LANES))
                place = yy * 64 + sign * 32
                turned = pltpu.roll(row, (place - (zz % 4) * 32 + LANES) % LANES, 1)
                total = jnp.where(lane8 // 32 == yy * 2 + sign, turned, total)
        vb[k] = total

    acc[...] = jnp.zeros_like(acc)
    x_copy.wait()
    for s in range(2):
        block = xv[partners[s] % occ_dev]
        for j in range(NOCC_AX):
            pieces[j, s] = block[:, j * LANES:(j + 1) * LANES]

    pl.semaphore_wait(barrier, len(peers))

    for j in range(1, NOCC_AX):
        to = (o + j) % NOCC_AX
        send(pieces.at[to], got.at[o], rs_send.at[to], rs_recv.at[o], occ_at(j)).start()
    got[o] = pieces[o]
    for j in range(1, NOCC_AX):
        source = (o + j) % NOCC_AX
        send(pieces.at[source], got.at[source], rs_send.at[source], rs_recv.at[source], occ_at(j)).wait_recv()
    for s in range(2):
        ybuf[0, c, s, y, x, 0] = got[partners[s] // occ_dev, s]

    mine_ref = ybuf.at[0, c, :, y, x, 0]

    def z_copy(k, sign, d):
        return send(mine_ref, ybuf.at[k, c, :, y, x, sign], z_send.at[k, sign], z_recv.at[k, sign], z_at(d))

    for j in range(1, PAIRS + 1):
        z_copy(j - 1, 1, -j).start()
        if j < PAIRS:
            z_copy(j, 0, j).start()

    def line_ref(k, phase, s, index):
        if phase == 0:
            return ybuf.at[k, c, 0, y, index] if s == 0 else ybuf.at[k, c, 1, index, x]
        return ybuf.at[k, c, 0, index] if s == 0 else ybuf.at[k, c, 1, :, index]

    def hop(k, phase, s, which):
        along_x = (phase + s) % 2 == 0
        pos, count, device = (x, NX, x_at) if along_x else (y, NY, y_at)
        s_sem, r_sem = (a_send, a_recv) if phase == 0 else (b_send, b_recv)
        if which == 2:
            ref = line_ref(k, phase, s, (pos - step_dir + count) % count)
            target = device(step_dir)
        else:
            ref = line_ref(k, phase, s, pos)
            target = device(1 - 2 * which)
        return send(ref, ref, s_sem.at[k, s, which], r_sem.at[k, s, which], target)

    def wait_hop(k, phase, s, which):
        along_x = (phase + s) % 2 == 0
        ref = line_ref(k, phase, s, x if along_x else y)
        s_sem, r_sem = (a_send, a_recv) if phase == 0 else (b_send, b_recv)
        send(ref, ref, s_sem.at[k, s, which], r_sem.at[k, s, which], x_at(1)).wait_recv()

    def twin(k):
        ref = ybuf.at[k, c]
        return send(ref, ref, c_send.at[k], c_recv.at[k], at(x, y, 1 - c, z))

    def first(k):
        @pl.when(k > 0)
        def _():
            z_copy(k, 0, 1).wait_recv()

        z_copy(k, 1, 1).wait_recv()
        for s in range(2):
            hop(k, 0, s, 0).start()
            hop(k, 0, s, 1).start()

    def second(k, phase):
        for s in range(2):
            wait_hop(k, phase, s, c)
            hop(k, phase, s, 2).start()

    def third(k):
        for s in range(2):
            wait_hop(k, 0, s, 1 - c)
            wait_hop(k, 0, s, 2)
            hop(k, 1, s, 0).start()
            hop(k, 1, s, 1).start()

    def fifth(k):
        for s in range(2):
            wait_hop(k, 1, s, 1 - c)
            wait_hop(k, 1, s, 2)
        twin(k).start()

    def tile(k, t):
        parts = []
        for s in range(2):
            for yy in range(2):
                halves = []
                for cc in range(2):
                    block = ybuf[k, cc, s, 2 * (t % 2) + yy, t // 2]
                    halves.append(block.reshape(2 * local_virt, LANES))
                parts.append(jnp.concatenate(halves, axis=1))
        return jnp.concatenate(parts, axis=0)

    def contract(k):
        scores = jnp.zeros((rows, 2 * LANES), F32)
        for t in range(aux // 256):
            left = xv[:, :, t * 256:(t + 1) * 256].reshape(rows, 256)
            scores += lax.dot_general(left, tile(k, t), (((1,), (1,)), ((), ())), preferred_element_type=F32)
        base = va[...] + vb[k][0:1, :] - own[...]
        amplitudes = jnp.concatenate(
            [
                (scores[:, s * LANES:(s + 1) * LANES] / (base - occ_energy[partners[s]])).astype(BF16)
                for s in range(2)
            ],
            axis=1,
        )
        for t in range(aux // 256):
            acc[:, t * 256:(t + 1) * 256] += jnp.dot(amplitudes, tile(k, t), preferred_element_type=F32)

    def sixth(k):
        send(ybuf.at[k, c], ybuf.at[k, 1 - c], c_send.at[k], c_recv.at[k], at(x, y, 1 - c, z)).wait_recv()
        contract(k)

    def tick(t, carry):
        def when(lag, run):
            @pl.when(jnp.logical_and(t >= lag, t < PAIRS + lag))
            def _():
                run(t - lag)

        when(4, fifth)
        when(3, lambda k: second(k, 1))
        when(2, third)
        when(1, lambda k: second(k, 0))
        when(0, first)
        when(5, sixth)
        return carry

    lax.fori_loop(0, PAIRS + STAGES, tick, 0)

    copies = []
    for t in range(aux // 512):
        cols = pl.ds(t * 512, 512)
        outv[:, :, cols] = acc[:, t * 512:(t + 1) * 512].reshape(occ_dev, local_virt, 512).astype(BF16)
        copy = pltpu.make_async_copy(outv.at[:, :, cols], out_hbm.at[:, :, cols], out_sem.at[t])
        copy.start()
        copies.append(copy)

    for j in range(1, NOCC_AX):
        to = (o + j) % NOCC_AX
        send(pieces.at[to], got.at[o], rs_send.at[to], rs_recv.at[o], occ_at(j)).wait_send()
    for j in range(1, PAIRS + 1):
        z_copy(j - 1, 1, -j).wait_send()
        if j < PAIRS:
            z_copy(j, 0, j).wait_send()

    def drain(k, carry):
        for phase in range(2):
            for s in range(2):
                for which in range(3):
                    hop(k, phase, s, which).wait_send()
        twin(k).wait_send()
        return carry

    lax.fori_loop(0, PAIRS, drain, 0)
    for copy in copies:
        copy.wait()


def per_device(integrals, occ_energy, virt_energy, partners):
    occ_dev, local_virt, aux = integrals.shape
    rows = occ_dev * local_virt
    dma = pltpu.SemaphoreType.DMA
    return pl.pallas_call(
        kernel,
        out_shape=jax.ShapeDtypeStruct(integrals.shape, BF16),
        in_specs=[
            pl.BlockSpec(memory_space=pltpu.SMEM),
            pl.BlockSpec(memory_space=pltpu.SMEM),
            pl.BlockSpec(memory_space=pltpu.VMEM),
            pl.BlockSpec(memory_space=pl.ANY),
        ],
        out_specs=pl.BlockSpec(memory_space=pl.ANY),
        scratch_shapes=[
            pltpu.VMEM(integrals.shape, BF16),
            pltpu.VMEM((NOCC_AX, 2, local_virt, LANES), BF16),
            pltpu.VMEM((NOCC_AX, 2, local_virt, LANES), BF16),
            pltpu.VMEM((PAIRS, NC, 2, NY, NX, 2, local_virt, LANES), BF16),
            pltpu.VMEM((rows, aux), F32),
            pltpu.VMEM(integrals.shape, BF16),
            pltpu.VMEM((rows, LANES), F32),
            pltpu.VMEM((rows, LANES), F32),
            pltpu.VMEM((PAIRS, 8, LANES), F32),
            dma, dma((aux // 512,)),
            dma((NOCC_AX,)), dma((NOCC_AX,)),
            dma((PAIRS, 2)), dma((PAIRS, 2)),
            dma((PAIRS, 2, 3)), dma((PAIRS, 2, 3)),
            dma((PAIRS, 2, 3)), dma((PAIRS, 2, 3)),
            dma((PAIRS,)), dma((PAIRS,)),
        ],
        compiler_params=pltpu.CompilerParams(collective_id=0, has_side_effects=True),
    )(partners, occ_energy, virt_energy.reshape(8, LANES), integrals)


def solution(mesh):
    in_specs = (P("occ", "virt", None), P(), P(), P())
    return jax.shard_map(
        per_device, mesh=mesh, in_specs=in_specs, out_specs=P("occ", "virt", None), check_vma=False
    )
```

time: 779 us -> 82.9 us (0.11)
  the two profiles are of different devices: /device:TPU:8 before, /device:TPU:1 now
where the time goes in v1:
time: 82.9 us; the launch traced here: 82.7 us
  Pallas kernels  79.9 us (96%)
  local copies, waits for them, and re-layouts  2.73 us (3%)
    pallas_call x1, Pallas kernels, per_device(): pl.pallas_call(kernel, out_shape=jax.ShapeDtypeStruct(integrals.shape, BF...  79.9 us
    unnamed x1, local copies, waits for them, and re-layouts  2.73 us

profile of v1, /device:TPU:1, one launch (start us, length us, event | category | flops | bytes accessed | tf_op | source)
XLA Modules:
  0.0 82.7 jit_solution(9795723932685519163)
XLA Ops:
  0.0 79.9 %shard_map.46 = bf16[12,32,2048]{2,1,0:T(8,128)(2,1)} custom-call(s32[2]{0:T(128)} %partners.1, f32[192]{0:T(256)} %occ_energy.1, f32[8,128]{1,0:T(8,128)} %bitcast.1, bf16[12,32,2048]{2,1,0:T(8,128)(2,1)} %x_hbm.1), custom_call_target="tpu_custom_call" | custom-call | tf_op jit(solution)/shard_map/pallas_call | solution.py:246
  79.9 2.7 %copy.6 = bf16[12,32,2048]{2,1,0:T(8,128)(2,1)} copy(bf16[12,32,2048]{2,1,0:T(8,128)(2,1)} %shard_map.46) | data formatting | bytes 3145728

commit v2 on v1

v2 whole, which is shorter than its diff:
```python
import jax
import jax.numpy as jnp
from jax import lax
from jax.experimental import pallas as pl
from jax.experimental.pallas import tpu as pltpu
from jax.sharding import PartitionSpec as P

MESH = pl.DeviceIdType.MESH
BF16, F32 = jnp.bfloat16, jnp.float32
NX, NY, NC, NZ = 4, 4, 2, 16
NOCC_AX = 16
LANES = 128
PAIRS = NZ // 2
STAGES = 5


def kernel(
    partners, occ_energy, virt_energy, x_hbm, out,
    xv, pieces, got, ybuf, acc, amp, va, own, vb,
    x_sem, rs_send, rs_recv, z_send, z_recv,
    a_send, a_recv, b_send, b_recv, c_send, c_recv,
):
    occ_dev, local_virt, aux = xv.shape
    rows = occ_dev * local_virt
    o, v = lax.axis_index("occ"), lax.axis_index("virt")
    x, yh, c = o // 4, (o // 2) % 2, o % 2
    yl, z = v // NZ, v % NZ
    y = 2 * yh + yl
    step_dir = 1 - 2 * c

    def at(xx, yy, cc, zz):
        return {"occ": (xx * 2 + yy // 2) * 2 + cc, "virt": (yy % 2) * NZ + zz}

    def send(src, dst, s_sem, r_sem, device):
        return pltpu.make_async_remote_copy(
            src_ref=src, dst_ref=dst, send_sem=s_sem, recv_sem=r_sem,
            device_id=device, device_id_type=MESH,
        )

    def x_at(d):
        return at((x + d + NX) % NX, y, c, z)

    def y_at(d):
        return at(x, (y + d + NY) % NY, c, z)

    def occ_at(j):
        return {"occ": (o + j) % NOCC_AX, "virt": v}

    def z_at(d):
        return at(x, y, c, (z + d + NZ) % NZ)

    x_copy = pltpu.make_async_copy(x_hbm, xv, x_sem)
    x_copy.start()

    barrier = pltpu.get_barrier_semaphore()
    peers = [occ_at(j) for j in range(1, NOCC_AX)]
    peers += [y_at(1), y_at(-1)]
    peers += [z_at(j) for j in range(1, NZ)]
    for peer in peers:
        pl.semaphore_signal(barrier, inc=1, device_id=peer, device_id_type=MESH)

    x_copy.wait()
    for s in range(2):
        block = xv[partners[s] % occ_dev]
        for j in range(NOCC_AX):
            pieces[j, s] = block[:, j * LANES:(j + 1) * LANES]

    pl.semaphore_wait(barrier, len(peers))

    for j in range(1, NOCC_AX):
        send(pieces.at[(o + j) % NOCC_AX], got.at[o], rs_send, rs_recv, occ_at(j)).start()
    got[o] = pieces[o]

    lane = lax.broadcasted_iota(jnp.int32, (local_virt, LANES), 1)
    sub = lax.broadcasted_iota(jnp.int32, (local_virt, LANES), 0)
    line = jnp.broadcast_to(virt_energy[pl.ds(v // 4, 1), :], (local_virt, LANES))
    mine = jnp.sum(jnp.where(lane == sub + (v % 4) * local_virt, line, 0.0), axis=1, keepdims=True)
    mine = jnp.broadcast_to(mine, (local_virt, LANES))
    for i in range(occ_dev):
        va[pl.ds(i * local_virt, local_virt), :] = mine
        own[pl.ds(i * local_virt, local_virt), :] = jnp.full((local_virt, LANES), occ_energy[o * occ_dev + i], F32)
    lane8 = lax.broadcasted_iota(jnp.int32, (8, LANES), 1)
    for k in range(PAIRS):
        total = jnp.zeros((8, LANES), F32)
        for yy in range(2):
            for sign in range(2):
                zz = (z + NZ - k) % NZ if sign == 0 else (z + k + 1) % NZ
                row = jnp.broadcast_to(virt_energy[pl.ds(yy * 4 + zz // 4, 1), :], (8, LANES))
                place = yy * 64 + sign * 32
                turned = pltpu.roll(row, (place - (zz % 4) * 32 + LANES) % LANES, 1)
                total = jnp.where(lane8 // 32 == yy * 2 + sign, turned, total)
        vb[k] = total
    acc[...] = jnp.zeros_like(acc)

    others = pieces.at[pl.ds(0, NOCC_AX - 1)]
    send(others, others, rs_send, rs_recv, occ_at(1)).wait_recv()
    for s in range(2):
        ybuf[0, c, s, y, x, 0] = got[partners[s] // occ_dev, s]

    mine_ref = ybuf.at[0, c, :, y, x, 0]

    def z_copy(k, sign, d):
        return send(mine_ref, ybuf.at[k, c, :, y, x, sign], z_send, z_recv.at[k], z_at(d))

    for j in range(1, PAIRS + 1):
        z_copy(j - 1, 1, -j).start()
        if j < PAIRS:
            z_copy(j, 0, j).start()

    def first(k):
        @pl.when(k > 0)
        def _():
            ref = pieces.at[pl.ds(0, 2)]
            send(ref, ref, z_send, z_recv.at[k], z_at(1)).wait_recv()

        @pl.when(k == 0)
        def _():
            ref = pieces.at[0]
            send(ref, ref, z_send, z_recv.at[k], z_at(1)).wait_recv()

        for d in (1, -1, 2):
            for s in range(2):
                ref = ybuf.at[k, c, s, y, x]
                send(ref, ref, a_send, a_recv.at[k], (y_at if s else x_at)(d)).start()

    def whole(k, s, index):
        return ybuf.at[k, c, 1, :, index] if s else ybuf.at[k, c, 0, index]

    def third(k):
        ref = ybuf.at[k, c, 0, pl.ds(0, 3), pl.ds(0, 2)]
        send(ref, ref, a_send, a_recv.at[k], x_at(1)).wait_recv()
        for s in range(2):
            ref = whole(k, s, x if s else y)
            to = x_at if s else y_at
            send(ref, ref, b_send, b_recv.at[k, 0], to(step_dir)).start()
            send(ref, ref, b_send, b_recv.at[k, 1], to(-step_dir)).start()

    def fourth(k):
        ref = ybuf.at[k, c, 0, pl.ds(0, 2)]
        send(ref, ref, b_send, b_recv.at[k, 0], x_at(1)).wait_recv()
        for s in range(2):
            ref = whole(k, s, ((x if s else y) - step_dir + 4) % 4)
            send(ref, ref, b_send, b_recv.at[k, 1], (x_at if s else y_at)(step_dir)).start()

    def fifth(k):
        ref = ybuf.at[k, c, 0]
        send(ref, ref, b_send, b_recv.at[k, 1], x_at(1)).wait_recv()
        ref = ybuf.at[k, c]
        send(ref, ref, c_send, c_recv.at[k], at(x, y, 1 - c, z)).start()

    def tile(k, t):
        parts = []
        for s in range(2):
            for yy in range(2):
                halves = []
                for cc in range(2):
                    block = ybuf[k, cc, s, 2 * (t % 2) + yy, t // 2]
                    halves.append(block.reshape(2 * local_virt, LANES))
                parts.append(jnp.concatenate(halves, axis=1))
        return jnp.concatenate(parts, axis=0)

    def score(k):
        send(ybuf.at[k, c], ybuf.at[k, 1 - c], c_send, c_recv.at[k], at(x, y, 1 - c, z)).wait_recv()
        scores = jnp.zeros((rows, 2 * LANES), F32)
        for t in range(aux // 256):
            left = xv[:, :, t * 256:(t + 1) * 256].reshape(rows, 256)
            scores += lax.dot_general(left, tile(k, t), (((1,), (1,)), ((), ())), preferred_element_type=F32)
        base = va[...] + vb[k][0:1, :] - own[...]
        for s in range(2):
            cols = slice(s * LANES, (s + 1) * LANES)
            amp[:, cols] = (scores[:, cols] / (base - occ_energy[partners[s]])).astype(BF16)

    def collect(k):
        for t in range(aux // 256):
            acc[:, t * 256:(t + 1) * 256] += jnp.dot(amp[...], tile(k, t), preferred_element_type=F32)

    def tick(t, carry):
        def when(lag, run):
            @pl.when(jnp.logical_and(t >= lag, t < PAIRS + lag))
            def _():
                run(t - lag)

        when(2, third)
        when(0, first)
        when(3, fourth)
        when(5, score)
        when(4, fifth)
        when(5, collect)
        return carry

    lax.fori_loop(0, PAIRS + STAGES, tick, 0)

    for t in range(aux // 256):
        cols = slice(t * 256, (t + 1) * 256)
        out[:, :, cols] = acc[:, cols].reshape(occ_dev, local_virt, 256).astype(BF16)

    for ref, sem in (
        (others, rs_send),
        (others, z_send),
        (ybuf.at[pl.ds(0, 3), 0, 0], a_send),
        (ybuf.at[pl.ds(0, 3)], b_send),
        (ybuf.at[pl.ds(0, 4)], c_send),
    ):
        send(ref, ref, sem, rs_recv, x_at(1)).wait_send()


def per_device(integrals, occ_energy, virt_energy, partners):
    occ_dev, local_virt, aux = integrals.shape
    rows = occ_dev * local_virt
    dma = pltpu.SemaphoreType.DMA
    return pl.pallas_call(
        kernel,
        out_shape=pltpu.VMEM(integrals.shape, BF16),
        in_specs=[
            pl.BlockSpec(memory_space=pltpu.SMEM),
            pl.BlockSpec(memory_space=pltpu.SMEM),
            pl.BlockSpec(memory_space=pltpu.VMEM),
            pl.BlockSpec(memory_space=pl.ANY),
        ],
        out_specs=pl.BlockSpec(memory_space=pltpu.VMEM),
        scratch_shapes=[
            pltpu.VMEM(integrals.shape, BF16),
            pltpu.VMEM((NOCC_AX, 2, local_virt, LANES), BF16),
            pltpu.VMEM((NOCC_AX, 2, local_virt, LANES), BF16),
            pltpu.VMEM((PAIRS, NC, 2, NY, NX, 2, local_virt, LANES), BF16),
            pltpu.VMEM((rows, aux), F32),
            pltpu.VMEM((rows, 2 * LANES), BF16),
            pltpu.VMEM((rows, LANES), F32),
            pltpu.VMEM((rows, LANES), F32),
            pltpu.VMEM((PAIRS, 8, LANES), F32),
            dma, dma, dma,
            dma, dma((PAIRS,)),
            dma, dma((PAIRS,)),
            dma, dma((PAIRS, 2)),
            dma, dma((PAIRS,)),
        ],
        compiler_params=pltpu.CompilerParams(collective_id=0, has_side_effects=True),
    )(partners, occ_energy, virt_energy.reshape(8, LANES), integrals)


def solution(mesh):
    in_specs = (P("occ", "virt", None), P(), P(), P())
    return jax.shard_map(
        per_device, mesh=mesh, in_specs=in_specs, out_specs=P("occ", "virt", None), check_vma=False
    )
```

time: 82.9 us -> 64.6 us (0.78)
  Pallas kernels: 79.9 us -> 63.2 us
  local copies, waits for them, and re-layouts: 2.73 us -> 1.15 us
    pallas_call x1, Pallas kernels: 79.9 us -> 63.2 us  [per_device(): pl.pallas_call(kernel, out_shape=pltpu.VMEM(integrals.shape, BF16), in_sp...]
    unnamed x1, local copies, waits for them, and re-layouts: 2.73 us -> 1.15 us
where the time goes in v2:
time: 64.6 us; the launch traced here: 64.4 us
  Pallas kernels  63.2 us (98%)
  local copies, waits for them, and re-layouts  1.15 us (2%)
    pallas_call x1, Pallas kernels, per_device(): pl.pallas_call(kernel, out_shape=pltpu.VMEM(integrals.shape, BF16), in_sp...  63.2 us

profile of v2, /device:TPU:1, one launch (start us, length us, event | category | flops | bytes accessed | tf_op | source)
XLA Modules:
  0.0 64.4 jit_solution(4151017348340496054)
XLA Ops:
  0.0 63.2 %shard_map.46 = bf16[12,32,2048]{2,1,0:T(8,128)(2,1)S(1)} custom-call(s32[2]{0:T(128)} %partners.1, f32[192]{0:T(256)} %occ_energy.1, f32[8,128]{1,0:T(8,128)} %bitcast.1, bf16[12,32,2048]{2,1,0:T(8,128)(2,1)} %x_hbm.1), custom_call_target="tpu_custom_call" | custom-call | tf_op jit(solution)/shard_map/pallas_call | solution.py:211
  63.3 1.1 %copy.6 = bf16[12,32,2048]{2,1,0:T(8,128)(2,1)} copy(bf16[12,32,2048]{2,1,0:T(8,128)(2,1)S(1)} %shard_map.46) | data formatting | bytes 3145728

commit v3 on v2

v3 whole, which is shorter than its diff:
```python
import jax
import jax.numpy as jnp
from jax import lax
from jax.experimental import pallas as pl
from jax.experimental.pallas import tpu as pltpu
from jax.sharding import PartitionSpec as P

MESH = pl.DeviceIdType.MESH
BF16, F32 = jnp.bfloat16, jnp.float32
NX, NY, NC, NZ = 4, 4, 2, 16
NOCC_AX = 16
LANES = 128
DISTANCE = (0, 1, 3, 5, 6, 7, 8, 2, 4)
SLOTS = len(DISTANCE)
LAST = 6


def kernel(
    partners_hbm, occ_hbm, virt_hbm, x_hbm, out,
    partners, occ_energy, virt_energy, xv, pieces, got, ybuf, acc, amp, va, own, vb, vh,
    x_sem, e_sem, rs_send, rs_recv, z_send, z_recv,
    a_send, a_recv, b_send, b_recv, c_send, c_recv, f_send, f_recv,
):
    occ_dev, local_virt, aux = xv.shape
    rows = occ_dev * local_virt
    o, v = lax.axis_index("occ"), lax.axis_index("virt")
    x, yh, c = o // 4, (o // 2) % 2, o % 2
    yl, z = v // NZ, v % NZ
    y = 2 * yh + yl
    step_dir = 1 - 2 * c

    def at(xx, yy, cc, zz):
        return {"occ": (xx * 2 + yy // 2) * 2 + cc, "virt": (yy % 2) * NZ + zz}

    def send(src, dst, s_sem, r_sem, device):
        return pltpu.make_async_remote_copy(
            src_ref=src, dst_ref=dst, send_sem=s_sem, recv_sem=r_sem,
            device_id=device, device_id_type=MESH,
        )

    def x_at(d):
        return at((x + d + NX) % NX, y, c, z)

    def y_at(d):
        return at(x, (y + d + NY) % NY, c, z)

    def member(dx, dyh, dc):
        return (((x + dx) % NX) * 2 + (yh + dyh) % 2) * 2 + (c + dc) % 2

    def z_at(d):
        return at(x, y, c, (z + d + NZ) % NZ)

    copies = [
        pltpu.make_async_copy(partners_hbm, partners, e_sem.at[0]),
        pltpu.make_async_copy(x_hbm, xv, x_sem),
        pltpu.make_async_copy(occ_hbm, occ_energy, e_sem.at[1]),
        pltpu.make_async_copy(virt_hbm, virt_energy, e_sem.at[2]),
    ]
    for copy in copies:
        copy.start()

    barrier = pltpu.get_barrier_semaphore()
    others = [(dx, dyh, dc) for dx, dyh in ((2, 1), (1, 1), (3, 1), (2, 0), (0, 1), (1, 0), (3, 0), (0, 0)) for dc in (0, 1)][:-2] + [(0, 0, 1)]
    peers = [{"occ": member(*d), "virt": v} for d in others[:-1]]
    peers += [z_at(sign * DISTANCE[u]) for u in (3, 2, 1) for sign in (1, -1)]
    peers += [y_at(1), y_at(-1), {"occ": member(0, 0, 1), "virt": v}]
    for peer in peers:
        pl.semaphore_signal(barrier, inc=1, device_id=peer, device_id_type=MESH)

    copies[0].wait()
    copies[1].wait()
    for s in range(2):
        block = xv[partners[s] % occ_dev]
        for j in range(NOCC_AX):
            pieces[j, s] = block[:, j * LANES:(j + 1) * LANES]

    pl.semaphore_wait(barrier, len(peers))

    for d in others:
        send(pieces.at[member(*d)], got.at[o], rs_send, rs_recv, {"occ": member(*d), "virt": v}).start()
    got[o] = pieces[o]

    copies[2].wait()
    copies[3].wait()
    lane = lax.broadcasted_iota(jnp.int32, (local_virt, LANES), 1)
    sub = lax.broadcasted_iota(jnp.int32, (local_virt, LANES), 0)
    line = jnp.broadcast_to(virt_energy[pl.ds(v // 4, 1), :], (local_virt, LANES))
    mine = jnp.sum(jnp.where(lane == sub + (v % 4) * local_virt, line, 0.0), axis=1, keepdims=True)
    mine = jnp.broadcast_to(mine, (local_virt, LANES))
    for i in range(occ_dev):
        va[pl.ds(i * local_virt, local_virt), :] = mine
        own[pl.ds(i * local_virt, local_virt), :] = jnp.full((local_virt, LANES), occ_energy[o * occ_dev + i], F32)
    lane8 = lax.broadcasted_iota(jnp.int32, (8, LANES), 1) // 32

    def turned(yy, zz, slot):
        row = jnp.broadcast_to(virt_energy[pl.ds(yy * 4 + zz // 4, 1), :], (8, LANES))
        return pltpu.roll(row, ((slot - zz % 4 + 4) % 4) * 32, 1)

    for u, d in enumerate(DISTANCE):
        if d in (0, NZ // 2):
            continue
        total = jnp.zeros((8, LANES), F32)
        for yy in range(2):
            for sign in range(2):
                zz = (z + d) % NZ if sign else (z + NZ - d) % NZ
                total = jnp.where(lane8 == yy * 2 + sign, turned(yy, zz, yy * 2 + sign), total)
        vb[u] = total
    for h in range(2):
        total = jnp.zeros((8, LANES), F32)
        for s in range(2):
            for yy in range(2):
                total = jnp.where(lane8 == s * 2 + yy, turned(yy, (z + 8 * h) % NZ, s * 2 + yy), total)
        vh[h] = total
    acc[...] = jnp.zeros_like(acc)

    fifteen = pieces.at[pl.ds(0, NOCC_AX - 1)]
    send(fifteen, fifteen, rs_send, rs_recv, x_at(1)).wait_recv()
    for s in range(2):
        ybuf[0, c, s, y, x, 0] = got[partners[s] // occ_dev, s]

    def z_copy(u, source, to, sign, d):
        return send(
            ybuf.at[u, c, :, y, x, source], ybuf.at[to, c, :, y, x, sign], z_send, z_recv.at[to], z_at(d)
        )

    def first(u, half):
        if half:
            @pl.when(u > 0)
            def _():
                ref = pieces.at[0]
                send(ref, ref, z_send, z_recv.at[u], z_at(1)).wait_recv()
        else:
            ref = pieces.at[pl.ds(0, 2)]
            send(ref, ref, z_send, z_recv.at[u], z_at(1)).wait_recv()

            @pl.when(u >= 3)
            def _():
                z_copy(u, 0, u + 1, 0, 1).start()

            @pl.when(jnp.logical_and(u >= 3, u < LAST - 1))
            def _():
                z_copy(u, 1, u + 1, 1, -1).start()

        for d in (1, -1, 2):
            for s in range(2):
                ref = ybuf.at[u, c, s, y, x, 0] if half else ybuf.at[u, c, s, y, x]
                send(ref, ref, a_send, a_recv.at[u], (y_at if s else x_at)(d)).start()

    def whole(u, half, s, index):
        if half:
            return ybuf.at[u, c, 1, :, index, 0] if s else ybuf.at[u, c, 0, index, :, 0]
        return ybuf.at[u, c, 1, :, index] if s else ybuf.at[u, c, 0, index]

    def third(u, half):
        six = ybuf.at[0, 0, 0, pl.ds(0, 3), pl.ds(0, 2), 0] if half else ybuf.at[0, 0, 0, pl.ds(0, 3), pl.ds(0, 2)]
        send(six, six, a_send, a_recv.at[u], x_at(1)).wait_recv()
        for s in range(2):
            ref = whole(u, half, s, x if s else y)
            to = x_at if s else y_at
            send(ref, ref, b_send, b_recv.at[u, 0], to(step_dir)).start()
            send(ref, ref, b_send, b_recv.at[u, 1], to(-step_dir)).start()

    def fourth(u, half):
        eight = ybuf.at[0, 0, 0, pl.ds(0, 2), :, 0] if half else ybuf.at[0, 0, 0, pl.ds(0, 2)]
        send(eight, eight, b_send, b_recv.at[u, 0], x_at(1)).wait_recv()
        for s in range(2):
            ref = whole(u, half, s, ((x if s else y) - step_dir + 4) % 4)
            send(ref, ref, b_send, b_recv.at[u, 1], (x_at if s else y_at)(step_dir)).start()

    def twin(u, half, core):
        ref = ybuf.at[u, core, :, :, :, 0] if half else ybuf.at[u, core]
        return send(ref, ref, c_send, c_recv.at[u], at(x, y, 1 - c, z))

    def fifth(u, half):
        sixteen = ybuf.at[0, 0, 0, :, :, 0] if half else ybuf.at[0, 0, 0]
        send(sixteen, sixteen, b_send, b_recv.at[u, 1], x_at(1)).wait_recv()
        twin(u, half, c).start()
        if not half:
            @pl.when(u < 3)
            def _():
                for sign in range(2):
                    send(
                        ybuf.at[u, c, :, :, :, sign], ybuf.at[u + LAST, c, :, :, :, sign],
                        f_send, f_recv.at[u], z_at(1 - 2 * sign),
                    ).start()

    def passed(u):
        send(ybuf.at[0, 0], ybuf.at[0, 0], f_send, f_recv.at[u - LAST], z_at(1)).wait_recv()
        twin(u, False, c).start()

    def tile(u, half, t):
        parts = []
        for s in range(2):
            for yy in range(2):
                halves = []
                for cc in range(2):
                    if half:
                        halves.append(ybuf[u, cc, s, 2 * (t % 2) + yy, t // 2, 0])
                    else:
                        halves.append(ybuf[u, cc, s, 2 * (t % 2) + yy, t // 2].reshape(2 * local_virt, LANES))
                parts.append(jnp.concatenate(halves, axis=1))
        return jnp.concatenate(parts, axis=0)

    def score(u, half):
        twin(u, half, 1 - c).wait_recv()
        width = LANES if half else 2 * LANES
        scores = jnp.zeros((rows, width), F32)
        for t in range(aux // 256):
            left = xv[:, :, t * 256:(t + 1) * 256].reshape(rows, 256)
            scores += lax.dot_general(left, tile(u, half, t), (((1,), (1,)), ((), ())), preferred_element_type=F32)
        line = vh[u // LAST] if half else vb[u]
        base = va[...] + line[0:1, :] - own[...]
        pair = [occ_energy[partners[s]] for s in range(2)]
        if half:
            both = jnp.where(lax.broadcasted_iota(jnp.int32, (1, LANES), 1) < 64, pair[0], pair[1])
            amp[:, :LANES] = (scores / (base - both)).astype(BF16)
        else:
            for s in range(2):
                cols = slice(s * LANES, (s + 1) * LANES)
                amp[:, cols] = (scores[:, cols] / (base - pair[s])).astype(BF16)

    def collect(u, half):
        for t in range(aux // 256):
            cols = slice(t * 256, (t + 1) * 256)
            left = amp[:, :LANES] if half else amp[...]
            acc[:, cols] += jnp.dot(left, tile(u, half, t), preferred_element_type=F32)

    for u in (1, 2, 3):
        for sign in range(2):
            z_copy(0, 0, u, sign, DISTANCE[u] * (1 - 2 * sign)).start()
    first(0, True)

    def tick(t, carry):
        def run_slot(u, run, also=True):
            @pl.when(jnp.logical_and(jnp.logical_and(u != 0, u != LAST), also))
            def _():
                run(u, False)

            @pl.when(jnp.logical_and(jnp.logical_or(u == 0, u == LAST), also))
            def _():
                run(u, True)

        def when(lag, run):
            run_slot(t - lag, run, jnp.logical_and(t >= lag, t <= LAST + lag))

        @pl.when(t <= LAST + 3)
        def _():
            when(2, third)
            when(3, fourth)

            @pl.when(t <= LAST)
            def _():
                run_slot(t, first)

        slot = jnp.where(t < 10, t - 5, jnp.where(t == 10, 7, jnp.where(t == 13, 8, t - 6)))
        run_slot(slot, score, t >= 5)

        @pl.when(t <= LAST + 4)
        def _():
            when(4, fifth)

        run_slot(slot, collect, t >= 5)
        for u in (7, 8):
            @pl.when(t == 2 * u - 6)
            def _():
                passed(u)

        return carry

    lax.fori_loop(1, 14, tick, 0)
    for t in range(aux // 256):
        cols = slice(t * 256, (t + 1) * 256)
        out[:, :, cols] = acc[:, cols].reshape(occ_dev, local_virt, 256).astype(BF16)

    for ref, sem in (
        (fifteen, rs_send),
        (pieces.at[pl.ds(0, 11)], z_send),
        (ybuf.at[pl.ds(0, 3), 0, 0, pl.ds(0, 3)], a_send),
        (ybuf.at[:, 0, 0], b_send),
        (ybuf.at[pl.ds(0, 4)], c_send),
        (ybuf.at[0], f_send),
    ):
        send(ref, ref, sem, rs_recv, x_at(1)).wait_send()


def per_device(integrals, occ_energy, virt_energy, partners):
    occ_dev, local_virt, aux = integrals.shape
    rows = occ_dev * local_virt
    dma = pltpu.SemaphoreType.DMA
    return pl.pallas_call(
        kernel,
        out_shape=pltpu.VMEM(integrals.shape, BF16),
        in_specs=[
            pl.BlockSpec(memory_space=pl.ANY),
            pl.BlockSpec(memory_space=pl.ANY),
            pl.BlockSpec(memory_space=pl.ANY),
            pl.BlockSpec(memory_space=pl.ANY),
        ],
        out_specs=pl.BlockSpec(memory_space=pltpu.VMEM),
        scratch_shapes=[
            pltpu.SMEM(partners.shape, partners.dtype),
            pltpu.SMEM(occ_energy.shape, F32),
            pltpu.VMEM((8, LANES), F32),
            pltpu.VMEM(integrals.shape, BF16),
            pltpu.VMEM((NOCC_AX, 2, local_virt, LANES), BF16),
            pltpu.VMEM((NOCC_AX, 2, local_virt, LANES), BF16),
            pltpu.VMEM((SLOTS, NC, 2, NY, NX, 2, local_virt, LANES), BF16),
            pltpu.VMEM((rows, aux), F32),
            pltpu.VMEM((rows, 2 * LANES), BF16),
            pltpu.VMEM((rows, LANES), F32),
            pltpu.VMEM((rows, LANES), F32),
            pltpu.VMEM((SLOTS, 8, LANES), F32),
            pltpu.VMEM((2, 8, LANES), F32),
            dma, dma((3,)),
            dma, dma,
            dma, dma((SLOTS,)),
            dma, dma((SLOTS,)),
            dma, dma((SLOTS, 2)),
            dma, dma((SLOTS,)),
            dma, dma((3,)),
        ],
        compiler_params=pltpu.CompilerParams(collective_id=0, has_side_effects=True),
    )(partners, occ_energy, virt_energy.reshape(8, LANES), integrals)


def solution(mesh):
    in_specs = (P("occ", "virt", None), P(), P(), P())
    return jax.shard_map(
        per_device, mesh=mesh, in_specs=in_specs, out_specs=P("occ", "virt", None), check_vma=False
    )
```

time: 64.6 us -> 56.6 us (0.88)
  Pallas kernels: 63.2 us -> 55.3 us
    pallas_call x1, Pallas kernels: 63.2 us -> 55.3 us  [per_device(): pl.pallas_call(kernel, out_shape=pltpu.VMEM(integrals.shape, BF16), in_sp...]
where the time goes in v3:
time: 56.6 us; the launch traced here: 56.4 us
  Pallas kernels  55.3 us (98%)
  local copies, waits for them, and re-layouts  1.15 us (2%)
    pallas_call x1, Pallas kernels, per_device(): pl.pallas_call(kernel, out_shape=pltpu.VMEM(integrals.shape, BF16), in_sp...  55.3 us
    unnamed x1, local copies, waits for them, and re-layouts  1.15 us

profile of v3, /device:TPU:1, one launch (start us, length us, event | category | flops | bytes accessed | tf_op | source)
XLA Modules:
  0.0 56.4 jit_solution(2158603432505777348)
XLA Ops:
  0.0 55.3 %shard_map.46 = bf16[12,32,2048]{2,1,0:T(8,128)(2,1)S(1)} custom-call(s32[2]{0:T(128)} %partners_hbm.1, f32[192]{0:T(256)} %occ_hbm.1, f32[8,128]{1,0:T(8,128)} %bitcast.1, bf16[12,32,2048]{2,1,0:T(8,128)(2,1)} %x_hbm.1), custom_call_target="tpu_custom_call" | custom-call | tf_op jit(solution)/shard_map/pallas_call | solution.py:290
  55.3 1.1 %copy.6 = bf16[12,32,2048]{2,1,0:T(8,128)(2,1)} copy(bf16[12,32,2048]{2,1,0:T(8,128)(2,1)S(1)} %shard_map.46) | data formatting | bytes 3145728

commit v4 on v3

--- a/solution.py
+++ b/solution.py
@@ -52,23 +52,28 @@
 
     copies = [
         pltpu.make_async_copy(partners_hbm, partners, e_sem.at[0]),
-        pltpu.make_async_copy(x_hbm, xv, x_sem),
         pltpu.make_async_copy(occ_hbm, occ_energy, e_sem.at[1]),
         pltpu.make_async_copy(virt_hbm, virt_energy, e_sem.at[2]),
     ]
-    for copy in copies:
+    third_of = occ_dev // 3
+    x_copies = [
+        pltpu.make_async_copy(x_hbm.at[pl.ds(i * third_of, third_of)], xv.at[pl.ds(i * third_of, third_of)], x_sem.at[i])
+        for i in range(3)
+    ]
+    for copy in x_copies + copies:
         copy.start()
 
     barrier = pltpu.get_barrier_semaphore()
     others = [(dx, dyh, dc) for dx, dyh in ((2, 1), (1, 1), (3, 1), (2, 0), (0, 1), (1, 0), (3, 0), (0, 0)) for dc in (0, 1)][:-2] + [(0, 0, 1)]
-    peers = [{"occ": member(*d), "virt": v} for d in others[:-1]]
-    peers += [z_at(sign * DISTANCE[u]) for u in (3, 2, 1) for sign in (1, -1)]
-    peers += [y_at(1), y_at(-1), {"occ": member(0, 0, 1), "virt": v}]
+    peers = [z_at(sign * d) for d in (3, 2) for sign in (1, -1)]
+    peers += [{"occ": member(*d), "virt": v} for d in others[:-1]]
+    peers += [z_at(1), z_at(-1), y_at(1), y_at(-1), {"occ": member(0, 0, 1), "virt": v}]
     for peer in peers:
         pl.semaphore_signal(barrier, inc=1, device_id=peer, device_id_type=MESH)
 
     copies[0].wait()
-    copies[1].wait()
+    for copy in x_copies:
+        copy.wait()
     for s in range(2):
         block = xv[partners[s] % occ_dev]
         for j in range(NOCC_AX):
@@ -80,8 +85,8 @@
         send(pieces.at[member(*d)], got.at[o], rs_send, rs_recv, {"occ": member(*d), "virt": v}).start()
     got[o] = pieces[o]
 
+    copies[1].wait()
     copies[2].wait()
-    copies[3].wait()
     lane = lax.broadcasted_iota(jnp.int32, (local_virt, LANES), 1)
     sub = lax.broadcasted_iota(jnp.int32, (local_virt, LANES), 0)
     line = jnp.broadcast_to(virt_energy[pl.ds(v // 4, 1), :], (local_virt, LANES))
@@ -133,15 +138,15 @@
             ref = pieces.at[pl.ds(0, 2)]
             send(ref, ref, z_send, z_recv.at[u], z_at(1)).wait_recv()
 
-            @pl.when(u >= 3)
-            def _():
-                z_copy(u, 0, u + 1, 0, 1).start()
-
-            @pl.when(jnp.logical_and(u >= 3, u < LAST - 1))
-            def _():
-                z_copy(u, 1, u + 1, 1, -1).start()
-
-        for d in (1, -1, 2):
+            for source, to in ((2, 3), (2, 4), (3, 5), (4, 6)):
+                @pl.when(u == source)
+                def _():
+                    hops = DISTANCE[to] - DISTANCE[source]
+                    z_copy(source, 0, to, 0, hops).start()
+                    if to < LAST:
+                        z_copy(source, 1, to, 1, -hops).start()
+
+        for d in (2, 1, -1):
             for s in range(2):
                 ref = ybuf.at[u, c, s, y, x, 0] if half else ybuf.at[u, c, s, y, x]
                 send(ref, ref, a_send, a_recv.at[u], (y_at if s else x_at)(d)).start()
@@ -225,7 +230,7 @@
             left = amp[:, :LANES] if half else amp[...]
             acc[:, cols] += jnp.dot(left, tile(u, half, t), preferred_element_type=F32)
 
-    for u in (1, 2, 3):
+    for u in (1, 2):
         for sign in range(2):
             z_copy(0, 0, u, sign, DISTANCE[u] * (1 - 2 * sign)).start()
     first(0, True)
@@ -311,11 +316,11 @@
             pltpu.VMEM((rows, LANES), F32),
             pltpu.VMEM((SLOTS, 8, LANES), F32),
             pltpu.VMEM((2, 8, LANES), F32),
-            dma, dma((3,)),
+            dma((3,)), dma((3,)),
             dma, dma,
-            dma, dma((SLOTS,)),
-            dma, dma((SLOTS,)),
-            dma, dma((SLOTS, 2)),
+            dma, dma((LAST + 1,)),
+            dma, dma((LAST + 1,)),
+            dma, dma((LAST + 1, 2)),
             dma, dma((SLOTS,)),
             dma, dma((3,)),
         ],

time: 56.6 us -> 54.3 us (0.959)
  Pallas kernels: 55.3 us -> 53 us
    pallas_call x1, Pallas kernels: 55.3 us -> 53 us  [per_device(): pl.pallas_call(kernel, out_shape=pltpu.VMEM(integrals.shape, BF16), in_sp...]
where the time goes in v4:
time: 54.3 us; the launch traced here: 54.1 us
  Pallas kernels  53 us (98%)
  local copies, waits for them, and re-layouts  1.15 us (2%)
    pallas_call x1, Pallas kernels, per_device(): pl.pallas_call(kernel, out_shape=pltpu.VMEM(integrals.shape, BF16), in_sp...  53 us
    unnamed x1, local copies, waits for them, and re-layouts  1.15 us

profile of v4, /device:TPU:1, one launch (start us, length us, event | category | flops | bytes accessed | tf_op | source)
XLA Modules:
  0.0 54.1 jit_solution(3121459607064046189)
XLA Ops:
  0.0 53.0 %shard_map.46 = bf16[12,32,2048]{2,1,0:T(8,128)(2,1)S(1)} custom-call(s32[2]{0:T(128)} %partners_hbm.1, f32[192]{0:T(256)} %occ_hbm.1, f32[8,128]{1,0:T(8,128)} %bitcast.1, bf16[12,32,2048]{2,1,0:T(8,128)(2,1)} %x_hbm.1), custom_call_target="tpu_custom_call" | custom-call | tf_op jit(solution)/shard_map/pallas_call | solution.py:295
  53.0 1.1 %copy.6 = bf16[12,32,2048]{2,1,0:T(8,128)(2,1)} copy(bf16[12,32,2048]{2,1,0:T(8,128)(2,1)S(1)} %shard_map.46) | data formatting | bytes 3145728

commit v5 on v4

--- a/solution.py
+++ b/solution.py
@@ -251,7 +251,7 @@
         @pl.when(t <= LAST + 3)
         def _():
             when(2, third)
-            when(3, fourth)
+            run_slot(t - 3, fourth, jnp.logical_and(t >= 3, t < LAST + 3))
 
             @pl.when(t <= LAST)
             def _():
@@ -259,6 +259,10 @@
 
         slot = jnp.where(t < 10, t - 5, jnp.where(t == 10, 7, jnp.where(t == 13, 8, t - 6)))
         run_slot(slot, score, t >= 5)
+
+        @pl.when(t == LAST + 3)
+        def _():
+            fourth(LAST, True)
 
         @pl.when(t <= LAST + 4)
         def _():

time: 54.3 us -> 55.8 us (1.028)
  Pallas kernels: 53 us -> 54.5 us
    pallas_call x1, Pallas kernels: 53 us -> 54.5 us  [per_device(): pl.pallas_call(kernel, out_shape=pltpu.VMEM(integrals.shape, BF16), in_sp...]
where the time goes in v5:
time: 55.8 us; the launch traced here: 55.7 us
  Pallas kernels  54.5 us (98%)
  local copies, waits for them, and re-layouts  1.15 us (2%)
    pallas_call x1, Pallas kernels, per_device(): pl.pallas_call(kernel, out_shape=pltpu.VMEM(integrals.shape, BF16), in_sp...  54.5 us
    unnamed x1, local copies, waits for them, and re-layouts  1.15 us

profile of v5, /device:TPU:1, one launch (start us, length us, event | category | flops | bytes accessed | tf_op | source)
XLA Modules:
  0.0 55.7 jit_solution(7471654118408701003)
XLA Ops:
  0.0 54.5 %shard_map.46 = bf16[12,32,2048]{2,1,0:T(8,128)(2,1)S(1)} custom-call(s32[2]{0:T(128)} %partners_hbm.1, f32[192]{0:T(256)} %occ_hbm.1, f32[8,128]{1,0:T(8,128)} %bitcast.1, bf16[12,32,2048]{2,1,0:T(8,128)(2,1)} %x_hbm.1), custom_call_target="tpu_custom_call" | custom-call | tf_op jit(solution)/shard_map/pallas_call | solution.py:299
  54.5 1.1 %copy.6 = bf16[12,32,2048]{2,1,0:T(8,128)(2,1)} copy(bf16[12,32,2048]{2,1,0:T(8,128)(2,1)S(1)} %shard_map.46) | data formatting | bytes 3145728

commit v6 on v4

--- a/solution.py
+++ b/solution.py
@@ -65,7 +65,7 @@
 
     barrier = pltpu.get_barrier_semaphore()
     others = [(dx, dyh, dc) for dx, dyh in ((2, 1), (1, 1), (3, 1), (2, 0), (0, 1), (1, 0), (3, 0), (0, 0)) for dc in (0, 1)][:-2] + [(0, 0, 1)]
-    peers = [z_at(sign * d) for d in (3, 2) for sign in (1, -1)]
+    peers = [z_at(sign * d) for d in (4, 3, 2) for sign in (1, -1)]
     peers += [{"occ": member(*d), "virt": v} for d in others[:-1]]
     peers += [z_at(1), z_at(-1), y_at(1), y_at(-1), {"occ": member(0, 0, 1), "virt": v}]
     for peer in peers:
@@ -138,7 +138,7 @@
             ref = pieces.at[pl.ds(0, 2)]
             send(ref, ref, z_send, z_recv.at[u], z_at(1)).wait_recv()
 
-            for source, to in ((2, 3), (2, 4), (3, 5), (4, 6)):
+            for source, to in ((1, 3), (2, 4), (3, 5), (4, 6)):
                 @pl.when(u == source)
                 def _():
                     hops = DISTANCE[to] - DISTANCE[source]

time: 54.3 us -> 54.8 us (level)
  no operation moved by 1% of the time
where the time goes in v6:
time: 54.8 us; the launch traced here: 54.7 us
  Pallas kernels  53.5 us (98%)
  local copies, waits for them, and re-layouts  1.15 us (2%)
    pallas_call x1, Pallas kernels, per_device(): pl.pallas_call(kernel, out_shape=pltpu.VMEM(integrals.shape, BF16), in_sp...  53.5 us
    unnamed x1, local copies, waits for them, and re-layouts  1.15 us

profile of v6, /device:TPU:1, one launch (start us, length us, event | category | flops | bytes accessed | tf_op | source)
XLA Modules:
  0.0 54.7 jit_solution(12667075119919759792)
XLA Ops:
  0.0 53.5 %shard_map.46 = bf16[12,32,2048]{2,1,0:T(8,128)(2,1)S(1)} custom-call(s32[2]{0:T(128)} %partners_hbm.1, f32[192]{0:T(256)} %occ_hbm.1, f32[8,128]{1,0:T(8,128)} %bitcast.1, bf16[12,32,2048]{2,1,0:T(8,128)(2,1)} %x_hbm.1), custom_call_target="tpu_custom_call" | custom-call | tf_op jit(solution)/shard_map/pallas_call | solution.py:295
  53.5 1.1 %copy.6 = bf16[12,32,2048]{2,1,0:T(8,128)(2,1)} copy(bf16[12,32,2048]{2,1,0:T(8,128)(2,1)S(1)} %shard_map.46) | data formatting | bytes 3145728
